TPU v7x, 32 devices: a whole 2x2x4 slice. The times are simulated.
32 devices in a mesh: ctx: 8 (over z, x), fsdp: 4 (over y, core).
Axes of the slice: x: 2, y: 2, z: 4, core: 2. Of those that a mesh axis runs over, the one named last changes fastest.
Arguments:
- tokens: bfloat16 [8, 1024, 768], P('fsdp', 'ctx'), may hold values from -6 to 6
- chars: bfloat16 [8, 1360, 768], P('fsdp', 'ctx'), may hold values from -6 to 6
- segment: int32 [8, 1024], P('fsdp', 'ctx'), may hold values from 0 to 3, as said below
- char_end: int32 [8, 1024], P('fsdp', 'ctx'), may hold values from 0 to 169, as said below
- w_qkv: bfloat16 [768, 2304], P('fsdp'), may hold values from -0.21875 to 0.21875
- w_out: bfloat16 [768, 768], P('fsdp'), may hold values from -4 to 4
- norm1_gain: bfloat16 [768], P('fsdp'), may hold values from 0.5 to 1.5
- norm1_bias: bfloat16 [768], P('fsdp'), may hold values from -1.796875 to 1.796875
- w_up: bfloat16 [768, 3072], P('fsdp'), may hold values from -0.21875 to 0.21875
- b_up: bfloat16 [3072], P('fsdp'), may hold values from -1.796875 to 1.796875
- w_down: bfloat16 [3072, 768], P('fsdp'), may hold values from -0.109375 to 0.109375
- norm2_gain: bfloat16 [768], P('fsdp'), may hold values from 0.5 to 1.5
- norm2_bias: bfloat16 [768], P('fsdp'), may hold values from -1.796875 to 1.796875
- w_gru: bfloat16 [768, 1536], P('fsdp'), may hold values from -0.21875 to 0.21875
- b_gate: bfloat16 [768], P('fsdp'), may hold values from 2.5 to 9
- w_ftok: bfloat16 [768, 768], P('fsdp'), may hold values from -0.21875 to 0.21875
- w_fchr: bfloat16 [768, 768], P('fsdp'), may hold values from -1.75 to 1.75
- w_conv: bfloat16 [3, 1536, 1536], P(None, 'fsdp'), may hold values from -0.09375 to 0.09375
- norm3_gain: bfloat16 [768], P('fsdp'), may hold values from 0.5 to 1.5
- norm3_bias: bfloat16 [768], P('fsdp'), may hold values from -1.796875 to 1.796875
- norm4_gain: bfloat16 [768], P('fsdp'), may hold values from 0.5 to 1.5
- norm4_bias: bfloat16 [768], P('fsdp'), may hold values from -1.796875 to 1.796875
- d_token: bfloat16 [8, 1024, 768], P('fsdp', 'ctx'), may hold values from -6 to 6
- d_char: bfloat16 [8, 1024, 768], P('fsdp', 'ctx'), may hold values from -6 to 6
Outputs:
- token_out: bfloat16 [8, 1024, 768], P('fsdp', 'ctx')
- char_out: bfloat16 [8, 1024, 768], P('fsdp', 'ctx')
- d_tokens: bfloat16 [8, 1024, 768], P('fsdp', 'ctx')
- d_chars: bfloat16 [8, 1360, 768], P('fsdp', 'ctx')
- qkv_grad: float32 [768, 2304], P('fsdp')
- wout_grad: float32 [768, 768], P('fsdp')
- gain1_grad: float32 [768], P('fsdp')
- bias1_grad: float32 [768], P('fsdp')
- up_grad: float32 [768, 3072], P('fsdp')
- bup_grad: float32 [3072], P('fsdp')
- down_grad: float32 [3072, 768], P('fsdp')
- gain2_grad: float32 [768], P('fsdp')
- bias2_grad: float32 [768], P('fsdp')
- gru_grad: float32 [768, 1536], P('fsdp')
- bgate_grad: float32 [768], P('fsdp')
- ftok_grad: float32 [768, 768], P('fsdp')
- fchr_grad: float32 [768, 768], P('fsdp')
- conv_grad: float32 [3, 1536, 1536], P(None, 'fsdp')
- gain3_grad: float32 [768], P('fsdp')
- bias3_grad: float32 [768], P('fsdp')
- gain4_grad: float32 [768], P('fsdp')
- bias4_grad: float32 [768], P('fsdp')
Inputs may be any that keep to these rules, and one draw needn't show every extreme that they name: Within each sequence the ids start at 0, never fall and rise by one where a new segment begins; the segment with id 1 begins on the first index of ctx and ends on the last, every other segment lies within the first or the last 128 tokens. `char_end`: each aligned block of 128 tokens (one index of ctx) owns the block of 170 characters at the same index; a token's value is its last character as an index within that block, strictly rising along the block, the block's last token ending at 169.
All inputs are finite; a program needn't handle non-finite values.
Results may differ from a plain program's by a relative error of at most 0.02.
Values may be sent and summed in bfloat16 or wider, within the bound.
No kernel may reach another device: no remote copies, remote signals or barrier semaphores. Data moves between devices by JAX's collectives and lax.ppermute only.
A program may use at most 320 MiB of HBM per device.

v0:
```python
from functools import partial

import jax
import jax.numpy as jnp
from jax import lax
from jax.sharding import PartitionSpec as P

HEADS = 12
HEAD_DIM = 64
GRU_H = 384


EPSILON = 1e-05
block_limit = 1024


def entering(value, axis, join, neutral, backward):
    count, mine = (lax.axis_size(axis), lax.axis_index(axis))
    pieces = jax.tree.map(lambda part: lax.all_gather(part, axis), value)
    if backward:
        pieces = jax.tree.map(lambda part: part[::-1], pieces)
        mine = count - 1 - mine
    so_far = jax.tree.map(
        lambda part, zero: jnp.full_like(part, 0) + jnp.asarray(zero, part.dtype), value, neutral
    )

    def hop(position, so_far):
        longer = join(so_far, jax.tree.map(lambda part: part[position], pieces))
        return jax.tree.map(lambda new, old: jnp.where(position < mine, new, old), longer, so_far)

    return lax.fori_loop(0, count - 1, hop, so_far)


def extended(x, sides, width):
    for axis, dim in sides:
        devices, length = (lax.axis_size(axis), x.shape[dim])
        up = [(i, (i + 1) % devices) for i in range(devices - 1)]
        down = [(j, i) for i, j in up]
        last = lax.slice_in_dim(x, length - width, length, axis=dim)
        first = lax.slice_in_dim(x, 0, width, axis=dim)
        before = lax.ppermute(last, axis, up)
        after = lax.ppermute(first, axis, down)
        x = jnp.concatenate([before, x, after], axis=dim)
    return x


def matmul(left, right):
    return jnp.dot(left, right, preferred_element_type=jnp.float32)


def matmul_nt(left, right):
    return lax.dot_general(
        left, right, (((1,), (1,)), ((), ())), preferred_element_type=jnp.float32
    )


def matmul_tn(left, right):
    return lax.dot_general(
        left, right, (((0,), (0,)), ((), ())), preferred_element_type=jnp.float32
    )


def layer_norm(value, gain, shift):
    center = value - jnp.mean(value, axis=-1, keepdims=True)
    inverse = lax.rsqrt(jnp.mean(center * center, axis=-1, keepdims=True) + EPSILON)
    return center * inverse * gain + shift


def chain(first, second):
    return (first[0] * second[0], second[0] * first[1] + second[1])


def gru_gates(columns, bias_part, reset):
    gate = jax.nn.sigmoid(columns[:, :GRU_H] + bias_part)
    return (gate * (1.0 - reset)[:, None], (1.0 - gate) * jnp.tanh(columns[:, GRU_H:]))


def block_size(rows):
    size = min(rows, block_limit)
    while rows % size != 0:
        size = size - 1
    return size


def split_blocks(array, size):
    return array.reshape((array.shape[0] // size, size) + array.shape[1:])


def to_heads(matrix):
    return matrix.reshape(matrix.shape[0], HEADS, HEAD_DIM)


def masked_exp(query_heads, key_heads, query_seg, key_seg):
    scores = jnp.einsum(
        "qhd,khd->hqk", query_heads, key_heads, preferred_element_type=jnp.float32
    ) * HEAD_DIM ** (-0.5)
    same = (query_seg[:, None] == key_seg[None, :])[None, :, :]
    return jnp.where(same, jnp.exp(scores), 0.0)


def forward_fold(query_heads, query_seg, my_start):

    def fold(carry, piece, start):
        key_rows, value_rows, key_seg = piece
        numer, total, prev_seg, next_seg = carry
        rows = key_rows.shape[0]
        size = block_size(rows)

        def step(acc, item):
            key_block, value_block, seg_block = item
            expvals = masked_exp(query_heads, to_heads(key_block), query_seg, seg_block)
            part_num = jnp.einsum(
                "hqk,khd->qhd",
                expvals.astype(jnp.bfloat16),
                to_heads(value_block),
                preferred_element_type=jnp.float32,
            )
            return ((acc[0] + part_num, acc[1] + jnp.transpose(jnp.sum(expvals, axis=-1))), None)

        (numer, total), unused = lax.scan(
            step,
            (numer, total),
            (
                split_blocks(key_rows, size),
                split_blocks(value_rows, size),
                split_blocks(key_seg, size),
            ),
        )
        before = my_start - 1
        after = my_start + query_seg.shape[0]
        prev_seg = jnp.where(
            (before >= 0) & (before < rows), key_seg[jnp.clip(before, 0, rows - 1)], prev_seg
        )
        next_seg = jnp.where(
            (after >= 0) & (after < rows), key_seg[jnp.clip(after, 0, rows - 1)], next_seg
        )
        return (numer, total, prev_seg, next_seg)

    return fold


def key_fold(key_heads, value_heads, key_seg, carry, piece):
    scale = HEAD_DIM ** (-0.5)
    query_rows, grad_rows, delta_rows, seg_rows = piece
    size = block_size(query_rows.shape[0])

    def step(acc, item):
        query_block, grad_block, delta_block, seg_block = item
        query_h = to_heads(query_block.astype(jnp.bfloat16))
        grad_h = to_heads(grad_block.astype(jnp.bfloat16))
        expvals = masked_exp(query_h, key_heads, seg_block, key_seg)
        dprob = jnp.einsum("qhd,khd->hqk", grad_h, value_heads, preferred_element_type=jnp.float32)
        dscore = (expvals * (dprob - jnp.transpose(delta_block)[:, :, None])).astype(jnp.bfloat16)
        dkey = (
            acc[0]
            + jnp.einsum("hqk,qhd->khd", dscore, query_h, preferred_element_type=jnp.float32)
            * scale
        )
        dval = acc[1] + jnp.einsum(
            "hqk,qhd->khd", expvals.astype(jnp.bfloat16), grad_h, preferred_element_type=jnp.float32
        )
        return ((dkey, dval), None)

    result, unused = lax.scan(
        step,
        carry,
        (
            split_blocks(query_rows, size),
            split_blocks(grad_rows, size),
            split_blocks(delta_rows, size),
            split_blocks(seg_rows, size),
        ),
    )
    return result


def query_fold(query_heads, grad_heads, delta, query_seg):
    scale = HEAD_DIM ** (-0.5)

    def fold(carry, piece, start):
        key_rows, value_rows, key_seg = piece
        size = block_size(key_rows.shape[0])

        def step(acc, item):
            key_block, value_block, seg_block = item
            key_h = to_heads(key_block)
            expvals = masked_exp(query_heads, key_h, query_seg, seg_block)
            dprob = jnp.einsum(
                "qhd,khd->hqk",
                grad_heads,
                to_heads(value_block),
                preferred_element_type=jnp.float32,
            )
            dscore = (expvals * (dprob - jnp.transpose(delta)[:, :, None])).astype(jnp.bfloat16)
            return (
                acc
                + jnp.einsum("hqk,khd->qhd", dscore, key_h, preferred_element_type=jnp.float32)
                * scale,
                None,
            )

        result, unused = lax.scan(
            step,
            carry,
            (
                split_blocks(key_rows, size),
                split_blocks(value_rows, size),
                split_blocks(key_seg, size),
            ),
        )
        return result

    return fold


def micro_step(weights, tok_in, chr_in, seg_row, end_row, dtok_row, dchr_row, my_start):
    (
        w_qkv,
        w_out,
        norm1_gain,
        norm1_bias,
        w_up,
        b_up,
        w_down,
        norm2_gain,
        norm2_bias,
        w_gru,
        b_gate,
        w_ftok,
        w_fchr,
        w_conv,
        norm3_gain,
        norm3_bias,
        norm4_gain,
        norm4_bias,
    ) = weights
    tok_rows = tok_in.shape[0]
    char_rows = chr_in.shape[0]
    width = tok_in.shape[1]
    identity = (jnp.ones((GRU_H,), jnp.float32), jnp.zeros((GRU_H,), jnp.float32))
    qkv = matmul(tok_in, w_qkv).astype(jnp.bfloat16)
    query_heads = to_heads(qkv[:, :width])
    key_rows = qkv[:, width : 2 * width]
    value_rows = qkv[:, 2 * width :]
    start_carry = (
        jnp.zeros((tok_rows, HEADS, HEAD_DIM), jnp.float32),
        jnp.zeros((tok_rows, HEADS), jnp.float32),
        jnp.int32(-1),
        jnp.int32(-1),
    )
    attend = forward_fold(query_heads, seg_row, my_start)
    numer, total, prev_seg, next_seg = attend(
        start_carry,
        (
            lax.all_gather(key_rows, "ctx", axis=0, tiled=True),
            lax.all_gather(value_rows, "ctx", axis=0, tiled=True),
            lax.all_gather(seg_row, "ctx", axis=0, tiled=True),
        ),
        jnp.int32(0),
    )
    context = numer / total[:, :, None]
    context_b = context.reshape(tok_rows, width).astype(jnp.bfloat16)
    attn = matmul(context_b, w_out)
    hidden1, norm1_back = jax.vjp(
        layer_norm,
        tok_in.astype(jnp.float32) + attn,
        norm1_gain.astype(jnp.float32),
        norm1_bias.astype(jnp.float32),
    )
    hidden1_b = hidden1.astype(jnp.bfloat16)
    pre = matmul(hidden1_b, w_up) + b_up.astype(jnp.float32)
    inner, gelu_back = jax.vjp(partial(jax.nn.gelu, approximate=False), pre)
    inner_b = inner.astype(jnp.bfloat16)
    ffn = matmul(inner_b, w_down)
    hidden2, norm2_back = jax.vjp(
        layer_norm, hidden1 + ffn, norm2_gain.astype(jnp.float32), norm2_bias.astype(jnp.float32)
    )
    tok_start = jnp.concatenate([jnp.zeros((1,), jnp.int32), end_row[:-1] + 1])
    seg_first = (seg_row != jnp.concatenate([prev_seg[None], seg_row[:-1]])).astype(jnp.float32)
    seg_last = (seg_row != jnp.concatenate([seg_row[1:], next_seg[None]])).astype(jnp.float32)
    char_pos = jnp.arange(char_rows, dtype=jnp.int32)
    char_first = jnp.sum(
        jnp.where(tok_start[:, None] == char_pos[None, :], seg_first[:, None], 0.0), axis=0
    )
    char_last = jnp.sum(
        jnp.where(end_row[:, None] == char_pos[None, :], seg_last[:, None], 0.0), axis=0
    )
    gate_in = matmul(chr_in, w_gru)
    bias_gate = b_gate.astype(jnp.float32)
    (fwd_decay, fwd_drive), fwd_back = jax.vjp(
        partial(gru_gates, reset=char_first), gate_in[:, : 2 * GRU_H], bias_gate[:GRU_H]
    )
    (bwd_decay, bwd_drive), bwd_back = jax.vjp(
        partial(gru_gates, reset=char_last), gate_in[:, 2 * GRU_H :], bias_gate[GRU_H:]
    )
    fwd_cum = lax.associative_scan(chain, (fwd_decay, fwd_drive))
    fwd_carry = entering((fwd_cum[0][-1], fwd_cum[1][-1]), "ctx", chain, identity, False)
    fwd_in = fwd_carry[1]
    fwd_state = fwd_cum[1] + fwd_cum[0] * fwd_in[None, :]
    bwd_cum = lax.associative_scan(chain, (bwd_decay[::-1], bwd_drive[::-1]))
    bwd_carry = entering((bwd_cum[0][-1], bwd_cum[1][-1]), "ctx", chain, identity, True)
    bwd_in = bwd_carry[1]
    bwd_state = (bwd_cum[1] + bwd_cum[0] * bwd_in[None, :])[::-1]
    char_tok = jnp.concatenate([fwd_state[end_row], bwd_state[tok_start]], axis=1)
    hidden2_b = hidden2.astype(jnp.bfloat16)
    char_tok_b = char_tok.astype(jnp.bfloat16)
    joined = jnp.concatenate(
        [matmul(hidden2_b, w_ftok), matmul(char_tok_b, w_fchr)], axis=1
    ).astype(jnp.bfloat16)
    padded = extended(joined, (("ctx", 0),), 1)
    conv = (
        matmul(padded[:-2], w_conv[0])
        + matmul(padded[1:-1], w_conv[1])
        + matmul(padded[2:], w_conv[2])
    )
    token_out, norm3_back = jax.vjp(
        layer_norm,
        hidden2 + conv[:, :width],
        norm3_gain.astype(jnp.float32),
        norm3_bias.astype(jnp.float32),
    )
    char_out, norm4_back = jax.vjp(
        layer_norm,
        char_tok + conv[:, width:],
        norm4_gain.astype(jnp.float32),
        norm4_bias.astype(jnp.float32),
    )
    d_in3, gain3_grad, bias3_grad = norm3_back(dtok_row.astype(jnp.float32))
    d_in4, gain4_grad, bias4_grad = norm4_back(dchr_row.astype(jnp.float32))
    d_conv = jnp.concatenate([d_in3, d_in4], axis=1).astype(jnp.bfloat16)
    d_padded = extended(d_conv, (("ctx", 0),), 1)
    d_joined = (
        matmul_nt(d_padded[2:], w_conv[0])
        + matmul_nt(d_padded[1:-1], w_conv[1])
        + matmul_nt(d_padded[:-2], w_conv[2])
    ).astype(jnp.bfloat16)
    conv_grad = jnp.stack(
        [
            matmul_tn(padded[:-2], d_conv),
            matmul_tn(padded[1:-1], d_conv),
            matmul_tn(padded[2:], d_conv),
        ]
    )
    ftok_grad = matmul_tn(hidden2_b, d_joined[:, :width])
    fchr_grad = matmul_tn(char_tok_b, d_joined[:, width:])
    d_hidden2 = d_in3 + matmul_nt(d_joined[:, :width], w_ftok)
    d_char_tok = d_in4 + matmul_nt(d_joined[:, width:], w_fchr)
    d_in2, gain2_grad, bias2_grad = norm2_back(d_hidden2)
    d_ffn = d_in2.astype(jnp.bfloat16)
    down_grad = matmul_tn(inner_b, d_ffn)
    (d_pre,) = gelu_back(matmul_nt(d_ffn, w_down))
    bup_grad = jnp.sum(d_pre, axis=0)
    d_pre_low = d_pre.astype(jnp.bfloat16)
    up_grad = matmul_tn(hidden1_b, d_pre_low)
    d_hidden1 = d_in2 + matmul_nt(d_pre_low, w_up)
    d_in1, gain1_grad, bias1_grad = norm1_back(d_hidden1)
    d_attn = d_in1.astype(jnp.bfloat16)
    wout_grad = matmul_tn(context_b, d_attn)
    d_context = matmul_nt(d_attn, w_out).reshape(tok_rows, HEADS, HEAD_DIM)
    grad_heads = (d_context / total[:, :, None]).astype(jnp.bfloat16)
    delta = jnp.sum(d_context * context, axis=-1) / total
    key_heads = to_heads(key_rows)
    value_heads = to_heads(value_rows)
    zero_heads = jnp.zeros((tok_rows, HEADS, HEAD_DIM), jnp.float32)
    query_send = qkv[:, :width].astype(jnp.float32)
    grad_send = grad_heads.reshape(tok_rows, width).astype(jnp.float32)
    dkey, dval = key_fold(
        key_heads,
        value_heads,
        seg_row,
        (zero_heads, zero_heads),
        (
            lax.all_gather(query_send.astype(jnp.bfloat16), "ctx", axis=0, tiled=True).astype(
                jnp.float32
            ),
            lax.all_gather(grad_send.astype(jnp.bfloat16), "ctx", axis=0, tiled=True).astype(
                jnp.float32
            ),
            lax.all_gather(delta.astype(jnp.bfloat16), "ctx", axis=0, tiled=True).astype(
                jnp.float32
            ),
            lax.all_gather(seg_row, "ctx", axis=0, tiled=True),
        ),
    )
    toward_query = query_fold(query_heads, grad_heads, delta, seg_row)
    dquery = toward_query(
        zero_heads,
        (
            lax.all_gather(key_rows, "ctx", axis=0, tiled=True),
            lax.all_gather(value_rows, "ctx", axis=0, tiled=True),
            lax.all_gather(seg_row, "ctx", axis=0, tiled=True),
        ),
        jnp.int32(0),
    )
    d_qkv = jnp.concatenate(
        [
            dquery.reshape(tok_rows, width),
            dkey.reshape(tok_rows, width),
            dval.reshape(tok_rows, width),
        ],
        axis=1,
    ).astype(jnp.bfloat16)
    qkv_grad = matmul_tn(tok_in, d_qkv)
    d_tokens = (d_in1 + matmul_nt(d_qkv, w_qkv)).astype(jnp.bfloat16)
    d_fwd = jnp.zeros((char_rows, GRU_H), jnp.float32).at[end_row].add(d_char_tok[:, :GRU_H])
    d_bwd = jnp.zeros((char_rows, GRU_H), jnp.float32).at[tok_start].add(d_char_tok[:, GRU_H:])
    adj_cum = lax.associative_scan(chain, (fwd_decay[::-1], (fwd_decay * d_fwd)[::-1]))
    adj_carry = entering((adj_cum[0][-1], adj_cum[1][-1]), "ctx", chain, identity, True)
    adj_in = adj_carry[1]
    carried = (adj_cum[1] + adj_cum[0] * adj_in[None, :])[::-1]
    fwd_adj = d_fwd + jnp.concatenate([carried[1:], adj_in[None, :]], axis=0)
    prev_state = jnp.concatenate([fwd_in[None, :], fwd_state[:-1]], axis=0)
    d_fcols, d_fbias = fwd_back((fwd_adj * prev_state, fwd_adj))
    badj_cum = lax.associative_scan(chain, (bwd_decay, bwd_decay * d_bwd))
    badj_carry = entering((badj_cum[0][-1], badj_cum[1][-1]), "ctx", chain, identity, False)
    badj_in = badj_carry[1]
    carried_left = badj_cum[1] + badj_cum[0] * badj_in[None, :]
    bwd_adj = d_bwd + jnp.concatenate([badj_in[None, :], carried_left[:-1]], axis=0)
    next_state = jnp.concatenate([bwd_state[1:], bwd_in[None, :]], axis=0)
    d_bcols, d_bbias = bwd_back((bwd_adj * next_state, bwd_adj))
    d_gate_in = jnp.concatenate([d_fcols, d_bcols], axis=1).astype(jnp.bfloat16)
    gru_grad = matmul_tn(chr_in, d_gate_in)
    bgate_grad = jnp.concatenate([d_fbias, d_bbias])
    d_chars = matmul_nt(d_gate_in, w_gru).astype(jnp.bfloat16)
    outputs = (token_out.astype(jnp.bfloat16), char_out.astype(jnp.bfloat16), d_tokens, d_chars)
    grads = (
        qkv_grad,
        wout_grad,
        gain1_grad,
        bias1_grad,
        up_grad,
        bup_grad,
        down_grad,
        gain2_grad,
        bias2_grad,
        gru_grad,
        bgate_grad,
        ftok_grad,
        fchr_grad,
        conv_grad,
        gain3_grad,
        bias3_grad,
        gain4_grad,
        bias4_grad,
    )
    return (outputs, grads)


def local(
    tokens,
    chars,
    segment,
    char_end,
    w_qkv,
    w_out,
    norm1_gain,
    norm1_bias,
    w_up,
    b_up,
    w_down,
    norm2_gain,
    norm2_bias,
    w_gru,
    b_gate,
    w_ftok,
    w_fchr,
    w_conv,
    norm3_gain,
    norm3_bias,
    norm4_gain,
    norm4_bias,
    d_token,
    d_char,
):
    micro_count = tokens.shape[0]
    my_start = lax.axis_index("ctx") * tokens.shape[1]
    token_list, char_list, dtok_list, dchr_list = ([], [], [], [])
    sums = None
    for micro in range(micro_count):
        whole = (
            lax.all_gather(w_qkv, "fsdp", axis=0, tiled=True),
            lax.all_gather(w_out, "fsdp", axis=0, tiled=True),
            lax.all_gather(norm1_gain, "fsdp", axis=0, tiled=True),
            lax.all_gather(norm1_bias, "fsdp", axis=0, tiled=True),
            lax.all_gather(w_up, "fsdp", axis=0, tiled=True),
            lax.all_gather(b_up, "fsdp", axis=0, tiled=True),
            lax.all_gather(w_down, "fsdp", axis=0, tiled=True),
            lax.all_gather(norm2_gain, "fsdp", axis=0, tiled=True),
            lax.all_gather(norm2_bias, "fsdp", axis=0, tiled=True),
            lax.all_gather(w_gru, "fsdp", axis=0, tiled=True),
            lax.all_gather(b_gate, "fsdp", axis=0, tiled=True),
            lax.all_gather(w_ftok, "fsdp", axis=0, tiled=True),
            lax.all_gather(w_fchr, "fsdp", axis=0, tiled=True),
            lax.all_gather(w_conv, "fsdp", axis=1, tiled=True),
            lax.all_gather(norm3_gain, "fsdp", axis=0, tiled=True),
            lax.all_gather(norm3_bias, "fsdp", axis=0, tiled=True),
            lax.all_gather(norm4_gain, "fsdp", axis=0, tiled=True),
            lax.all_gather(norm4_bias, "fsdp", axis=0, tiled=True),
        )
        outputs, grads = micro_step(
            whole,
            tokens[micro],
            chars[micro],
            segment[micro],
            char_end[micro],
            d_token[micro],
            d_char[micro],
            my_start,
        )
        token_list.append(outputs[0])
        char_list.append(outputs[1])
        dtok_list.append(outputs[2])
        dchr_list.append(outputs[3])
        sums = (
            grads if sums is None else tuple((running + grad for running, grad in zip(sums, grads)))
        )
    shares = (
        lax.psum_scatter(
            sums[0].astype(jnp.bfloat16), "fsdp", scatter_dimension=0, tiled=True
        ).astype(jnp.float32),
        lax.psum_scatter(
            sums[1].astype(jnp.bfloat16), "fsdp", scatter_dimension=0, tiled=True
        ).astype(jnp.float32),
        lax.psum_scatter(
            sums[2].astype(jnp.bfloat16), "fsdp", scatter_dimension=0, tiled=True
        ).astype(jnp.float32),
        lax.psum_scatter(
            sums[3].astype(jnp.bfloat16), "fsdp", scatter_dimension=0, tiled=True
        ).astype(jnp.float32),
        lax.psum_scatter(
            sums[4].astype(jnp.bfloat16), "fsdp", scatter_dimension=0, tiled=True
        ).astype(jnp.float32),
        lax.psum_scatter(
            sums[5].astype(jnp.bfloat16), "fsdp", scatter_dimension=0, tiled=True
        ).astype(jnp.float32),
        lax.psum_scatter(
            sums[6].astype(jnp.bfloat16), "fsdp", scatter_dimension=0, tiled=True
        ).astype(jnp.float32),
        lax.psum_scatter(
            sums[7].astype(jnp.bfloat16), "fsdp", scatter_dimension=0, tiled=True
        ).astype(jnp.float32),
        lax.psum_scatter(
            sums[8].astype(jnp.bfloat16), "fsdp", scatter_dimension=0, tiled=True
        ).astype(jnp.float32),
        lax.psum_scatter(
            sums[9].astype(jnp.bfloat16), "fsdp", scatter_dimension=0, tiled=True
        ).astype(jnp.float32),
        lax.psum_scatter(
            sums[10].astype(jnp.bfloat16), "fsdp", scatter_dimension=0, tiled=True
        ).astype(jnp.float32),
        lax.psum_scatter(
            sums[11].astype(jnp.bfloat16), "fsdp", scatter_dimension=0, tiled=True
        ).astype(jnp.float32),
        lax.psum_scatter(
            sums[12].astype(jnp.bfloat16), "fsdp", scatter_dimension=0, tiled=True
        ).astype(jnp.float32),
        lax.psum_scatter(
            sums[13].astype(jnp.bfloat16), "fsdp", scatter_dimension=1, tiled=True
        ).astype(jnp.float32),
        lax.psum_scatter(
            sums[14].astype(jnp.bfloat16), "fsdp", scatter_dimension=0, tiled=True
        ).astype(jnp.float32),
        lax.psum_scatter(
            sums[15].astype(jnp.bfloat16), "fsdp", scatter_dimension=0, tiled=True
        ).astype(jnp.float32),
        lax.psum_scatter(
            sums[16].astype(jnp.bfloat16), "fsdp", scatter_dimension=0, tiled=True
        ).astype(jnp.float32),
        lax.psum_scatter(
            sums[17].astype(jnp.bfloat16), "fsdp", scatter_dimension=0, tiled=True
        ).astype(jnp.float32),
    )
    totals = lax.psum(
        (
            shares[0],
            shares[1],
            shares[2],
            shares[3],
            shares[4],
            shares[5],
            shares[6],
            shares[7],
            shares[8],
            shares[9],
            shares[10],
            shares[11],
            shares[12],
            shares[13],
            shares[14],
            shares[15],
            shares[16],
            shares[17],
        ),
        "ctx",
    )
    return (
        jnp.stack(token_list),
        jnp.stack(char_list),
        jnp.stack(dtok_list),
        jnp.stack(dchr_list),
        totals[0],
        totals[1],
        totals[2],
        totals[3],
        totals[4],
        totals[5],
        totals[6],
        totals[7],
        totals[8],
        totals[9],
        totals[10],
        totals[11],
        totals[12],
        totals[13],
        totals[14],
        totals[15],
        totals[16],
        totals[17],
    )


def solution(mesh):
    return jax.shard_map(
        local,
        mesh=mesh,
        in_specs=(
            P("fsdp", "ctx", None),
            P("fsdp", "ctx", None),
            P("fsdp", "ctx"),
            P("fsdp", "ctx"),
            P("fsdp", None),
            P("fsdp", None),
            P("fsdp"),
            P("fsdp"),
            P("fsdp", None),
            P("fsdp"),
            P("fsdp", None),
            P("fsdp"),
            P("fsdp"),
            P("fsdp", None),
            P("fsdp"),
            P("fsdp", None),
            P("fsdp", None),
            P(None, "fsdp", None),
            P("fsdp"),
            P("fsdp"),
            P("fsdp"),
            P("fsdp"),
            P("fsdp", "ctx", None),
            P("fsdp", "ctx", None),
        ),
        out_specs=(
            P("fsdp", "ctx", None),
            P("fsdp", "ctx", None),
            P("fsdp", "ctx", None),
            P("fsdp", "ctx", None),
            P("fsdp", None),
            P("fsdp", None),
            P("fsdp"),
            P("fsdp"),
            P("fsdp", None),
            P("fsdp"),
            P("fsdp", None),
            P("fsdp"),
            P("fsdp"),
            P("fsdp", None),
            P("fsdp"),
            P("fsdp", None),
            P("fsdp", None),
            P(None, "fsdp", None),
            P("fsdp"),
            P("fsdp"),
            P("fsdp"),
            P("fsdp"),
        ),
        check_vma=False,
    )
```

profile of v0, /device:TPU:0, one launch (start us, length us, event | category | flops | bytes accessed | tf_op | source)
XLA Modules:
  0.0 2174.5 jit_solution(9931954615823727211)
XLA Ops:
  9.5 33.6 %all-gather.36.cloned.1.call-done = bf16[768,2304]{1,0:T(8,128)(2,1)} async-done(((bf16[192,2304]{1,0:T(8,128)(2,1)}), bf16[768,2304]{1,0:T(8,128)(2,1)}) %all-gather.36.cloned.1.call-update) | async-done | bytes 3538960 | tf_op jit(solution)/shard_map/all_gather | solution.py:481
  58.2 10.8 all-reduce.253
  69.0 20.7 all-gather.1
  89.7 16.2 all-gather
  111.1 5.3 all-gather.2
  214.2 26.2 %all-gather.3 = f32[8,1,384]{2,1,0:T(1,128)S(1)} all-gather(f32[1,1,384]{2,1,0:T(1,128)S(1)} %add_bitcast_fusion.15), channel_id=1, replica_groups=mesh['ctx'=8,'fsdp'=4] {'ctx'}, dimensions={0}, use_global_device_ids=true | all-gather | bytes 13824 | tf_op jit(solution)/shard_map/all_gather | solution.py:19
  241.0 26.1 %all-gather.4 = f32[8,1,384]{2,1,0:T(1,128)S(1)} all-gather(f32[1,1,384]{2,1,0:T(1,128)S(1)} %add_bitcast_fusion.14), channel_id=1, replica_groups=mesh['ctx'=8,'fsdp'=4] {'ctx'}, dimensions={0}, use_global_device_ids=true | all-gather | bytes 13824 | tf_op jit(solution)/shard_map/all_gather | solution.py:19
  274.8 25.9 %all-gather.5 = f32[8,1,384]{2,1,0:T(1,128)S(1)} all-gather(f32[1,1,384]{2,1,0:T(1,128)S(1)} %add_bitcast_fusion.13), channel_id=1, replica_groups=mesh['ctx'=8,'fsdp'=4] {'ctx'}, dimensions={0}, use_global_device_ids=true | all-gather | bytes 13824 | tf_op jit(solution)/shard_map/all_gather | solution.py:19
  300.8 25.9 %all-gather.6 = f32[8,1,384]{2,1,0:T(1,128)S(1)} all-gather(f32[1,1,384]{2,1,0:T(1,128)S(1)} %add_bitcast_fusion.12), channel_id=1, replica_groups=mesh['ctx'=8,'fsdp'=4] {'ctx'}, dimensions={0}, use_global_device_ids=true | all-gather | bytes 13824 | tf_op jit(solution)/shard_map/all_gather | solution.py:19
  332.5 25.9 %all-gather.7 = f32[8,1,384]{2,1,0:T(1,128)S(1)} all-gather(f32[1,1,384]{2,1,0:T(1,128)S(1)} %add_bitcast_fusion.11), channel_id=1, replica_groups=mesh['ctx'=8,'fsdp'=4] {'ctx'}, dimensions={0}, use_global_device_ids=true | all-gather | bytes 13824 | tf_op jit(solution)/shard_map/all_gather | solution.py:19
  359.0 26.3 %all-gather.8 = f32[8,1,384]{2,1,0:T(1,128)S(1)} all-gather(f32[1,1,384]{2,1,0:T(1,128)S(1)} %add_bitcast_fusion.10), channel_id=1, replica_groups=mesh['ctx'=8,'fsdp'=4] {'ctx'}, dimensions={0}, use_global_device_ids=true | all-gather | bytes 13824 | tf_op jit(solution)/shard_map/all_gather | solution.py:19
  415.1 26.0 %all-gather.9 = f32[8,1,384]{2,1,0:T(1,128)S(1)} all-gather(f32[1,1,384]{2,1,0:T(1,128)S(1)} %add_bitcast_fusion.9), channel_id=1, replica_groups=mesh['ctx'=8,'fsdp'=4] {'ctx'}, dimensions={0}, use_global_device_ids=true | all-gather | bytes 13824 | tf_op jit(solution)/shard_map/all_gather | solution.py:19
  442.4 25.9 %all-gather.10 = f32[8,1,384]{2,1,0:T(1,128)S(1)} all-gather(f32[1,1,384]{2,1,0:T(1,128)S(1)} %add_bitcast_fusion.8), channel_id=1, replica_groups=mesh['ctx'=8,'fsdp'=4] {'ctx'}, dimensions={0}, use_global_device_ids=true | all-gather | bytes 13824 | tf_op jit(solution)/shard_map/all_gather | solution.py:19
  469.5 5.5 while.143
  479.3 5.5 while.140
  488.8 5.5 while.142
  506.8 6.0 fusion.4
  515.4 5.3 fusion.388
  526.0 5.8 fusion.6
  534.4 5.4 fusion.391
  540.9 8.6 multiply_convert_fusion.9
  549.6 6.4 multiply_convert_fusion.8
  566.9 5.1 collective-permute-start
  575.9 5.1 collective-permute-start.2
  590.7 3.9 fusion.43
  611.4 5.1 collective-permute-start.7
  769.8 5.1 fusion.44
  821.2 4.6 fusion.66
  875.5 5.7 fusion.394
  884.2 26.2 %all-gather.17 = f32[8,1,384]{2,1,0:T(1,128)S(1)} all-gather(f32[1,1,384]{2,1,0:T(1,128)S(1)} %add_bitcast_fusion.1), channel_id=1, replica_groups=mesh['ctx'=8,'fsdp'=4] {'ctx'}, dimensions={0}, use_global_device_ids=true | all-gather | bytes 13824 | tf_op jit(solution)/shard_map/all_gather | solution.py:19
  911.0 26.1 %all-gather.18 = f32[8,1,384]{2,1,0:T(1,128)S(1)} all-gather(f32[1,1,384]{2,1,0:T(1,128)S(1)} %add_bitcast_fusion), channel_id=1, replica_groups=mesh['ctx'=8,'fsdp'=4] {'ctx'}, dimensions={0}, use_global_device_ids=true | all-gather | bytes 13824 | tf_op jit(solution)/shard_map/all_gather | solution.py:19
  937.7 4.2 convolution_add_fusion.11
  942.0 5.3 fusion.395
  960.5 13.7 while.147
  978.2 26.4 %all-gather.13 = f32[8,1,384]{2,1,0:T(1,128)S(1)} all-gather(f32[1,1,384]{2,1,0:T(1,128)} %add_bitcast_fusion.5), channel_id=1, replica_groups=mesh['ctx'=8,'fsdp'=4] {'ctx'}, dimensions={0}, use_global_device_ids=true | all-gather | bytes 13824 | tf_op jit(solution)/shard_map/all_gather | solution.py:19
  1004.6 26.0 %all-gather.14 = f32[8,1,384]{2,1,0:T(1,128)S(1)} all-gather(f32[1,1,384]{2,1,0:T(1,128)S(1)} %copy-done.384), channel_id=1, replica_groups=mesh['ctx'=8,'fsdp'=4] {'ctx'}, dimensions={0}, use_global_device_ids=true | all-gather | bytes 13824 | tf_op jit(solution)/shard_map/all_gather | solution.py:19
  1030.7 25.9 %all-gather.11 = f32[8,1,384]{2,1,0:T(1,128)S(1)} all-gather(f32[1,1,384]{2,1,0:T(1,128)S(1)} %copy-done.383), channel_id=1, replica_groups=mesh['ctx'=8,'fsdp'=4] {'ctx'}, dimensions={0}, use_global_device_ids=true | all-gather | bytes 13824 | tf_op jit(solution)/shard_map/all_gather | solution.py:19
  1057.5 25.9 %all-gather.12 = f32[8,1,384]{2,1,0:T(1,128)S(1)} all-gather(f32[1,1,384]{2,1,0:T(1,128)S(1)} %add_bitcast_fusion.6), channel_id=1, replica_groups=mesh['ctx'=8,'fsdp'=4] {'ctx'}, dimensions={0}, use_global_device_ids=true | all-gather | bytes 13824 | tf_op jit(solution)/shard_map/all_gather | solution.py:19
  1084.8 25.9 %all-gather.15 = f32[8,1,384]{2,1,0:T(1,128)S(1)} all-gather(f32[1,1,384]{2,1,0:T(1,128)S(1)} %add_bitcast_fusion.3), channel_id=1, replica_groups=mesh['ctx'=8,'fsdp'=4] {'ctx'}, dimensions={0}, use_global_device_ids=true | all-gather | bytes 13824 | tf_op jit(solution)/shard_map/all_gather | solution.py:19
  1115.8 25.9 %all-gather.16 = f32[8,1,384]{2,1,0:T(1,128)S(1)} all-gather(f32[1,1,384]{2,1,0:T(1,128)S(1)} %add_bitcast_fusion.2), channel_id=1, replica_groups=mesh['ctx'=8,'fsdp'=4] {'ctx'}, dimensions={0}, use_global_device_ids=true | all-gather | bytes 13824 | tf_op jit(solution)/shard_map/all_gather | solution.py:19
  1161.0 3.9 slice.2345
  1173.3 4.3 copy.140
  1180.3 3.8 add_convert_fusion.1
  1209.7 26.0 %all_gather.201 = bf16[1024,12]{0,1:T(8,128)(2,1)S(1)} all-gather(bf16[128,12]{0,1:T(8,128)(2,1)S(1)} %divide_convert_fusion.8), channel_id=1, replica_groups=mesh['ctx'=8,'fsdp'=4] {'ctx'}, dimensions={0}, use_global_device_ids=true | all-gather | bytes 27648 | tf_op jit(solution)/shard_map/all_gather | solution.py:379
  1236.8 26.0 %all_gather.198 = bf16[1024,12]{0,1:T(8,128)(2,1)S(1)} all-gather(bf16[128,12]{0,1:T(8,128)(2,1)S(1)} %divide_convert_fusion.9), channel_id=1, replica_groups=mesh['ctx'=8,'fsdp'=4] {'ctx'}, dimensions={0}, use_global_device_ids=true | all-gather | bytes 27648 | tf_op jit(solution)/shard_map/all_gather | solution.py:379
  1265.3 7.2 fusion.91
  1272.5 7.2 fusion.89
  1285.1 5.3 fusion.93
  1290.4 8.0 fusion.90
  1298.4 5.3 fusion.181
  1303.7 5.3 fusion.96
  1309.0 6.3 fusion.92
  1315.3 4.4 fusion.3
  1319.8 3.8 copy.138
  1324.8 5.1 convolution_bitcast_fusion.4
  1329.9 5.0 convolution_bitcast_fusion.1
  1334.9 5.7 convolution_bitcast_fusion.3
  1340.5 6.4 convolution_bitcast_fusion.5
  1347.0 5.7 convolution_bitcast_fusion
  1352.6 5.7 convolution_bitcast_fusion.2
  1358.4 23.7 %fusion = bf16[3,1536,1536]{2,1,0:T(8,128)(2,1)} fusion(f32[1,1536,1536]{2,1,0:T(8,128)} %convolution_bitcast_fusion.3, f32[1,1536,1536]{2,1,0:T(8,128)} %convolution_bitcast_fusion.4, f32[1,1536,1536]{2,1,0:T(8,128)} %convolution_bitcast_fusion.5, f32[1,1536,1536]{2,1,0:T(8,128)} %convolution_bitcast_fusion, f32[1,1536,1536]{2,1,0:T(8,128)} %convolution_bitcast_fusion.1, ...), kind=kLoop, calls=%fused_computation.33 | loop fusion | flops 42467328 | bytes 70778880 | tf_op jit(solution)/shard_map/convert_element_type | solution.py:558
  1384.8 10.5 all-reduce.252
  1414.3 75.0 %reduce-scatter.23.cloned.1.call-done = bf16[3,384,1536]{2,1,0:T(8,128)(2,1)} async-done(((bf16[3,1536,1536]{2,1,0:T(8,128)(2,1)}), bf16[3,384,1536]{2,1,0:T(8,128)(2,1)}) %reduce-scatter.23.cloned.1.call-update) | async-done | bytes 3538960 | tf_op jit(solution)/shard_map/reduce_scatter | solution.py:557
  1489.3 673.8 %all-reduce.255 = (f32[192,2304]{0,1:T(8,128)}, f32[192,768]{1,0:T(8,128)}, f32[192]{0:T(256)}, f32[192]{0:T(256)}, f32[192,3072]{1,0:T(8,128)}, /*index=5*/f32[...) all-reduce(bf16[192,2304]{0,1:T(8,128)(2,1)S(1)} %copy.139, ...), channel_id=1, replica_groups=mesh['ctx'=8,'fsdp'=4] {'ctx'}, use_global_device_ids=true, to_apply=%region_61.62 | all-reduce | flops 4131264 | bytes 24792576 | tf_op jit(solution)/shard_map/psum | solution.py:573
  (2278 shorter events, 628.3 us)
Async XLA Ops:
  7.2 35.9 %all-gather.36.cloned.1.call-start = ((), (), s32[]{:S(2)}) async-start(), calls=%async_computation.8 | async-start | bytes 4423680 | tf_op jit(solution)/shard_map/all_gather | solution.py:481
  7.9 114.9 %all-gather.50.cloned.1.call-start = ((), (), s32[]{:S(2)}) async-start(), calls=%async_computation.15 | async-start | bytes 2949120 | tf_op jit(solution)/shard_map/all_gather | solution.py:490
  8.7 492.3 %all-gather.52.cloned.1.call-start = ((), (), s32[]{:S(2)}) async-start(), calls=%async_computation.16 | async-start | bytes 1474560 | tf_op jit(solution)/shard_map/all_gather | solution.py:493
  9.4 495.6 %all-gather.40.cloned.1.call-start = ((), (), s32[]{:S(2)}) async-start(), calls=%async_computation.10 | async-start | bytes 1769472 | tf_op jit(solution)/shard_map/all_gather | solution.py:255
  46.9 466.0 %all-gather.38.cloned.1.call-start = ((), (), s32[]{:S(2)}) async-start(), calls=%async_computation.9 | async-start | bytes 1769472 | tf_op jit(solution)/shard_map/all_gather | solution.py:256
  47.4 473.3 %all-gather.42.cloned.1.call-start = ((), (), s32[]{:S(2)}) async-start(), calls=%async_computation.11 | async-start | bytes 1474560 | tf_op jit(solution)/shard_map/all_gather | solution.py:482
  48.0 475.3 %all-gather.58.cloned.1.call-start = ((), (), s32[]{:S(2)}) async-start(), calls=%async_computation.19 | async-start | bytes 1769472 | tf_op jit(solution)/shard_map/all_gather | solution.py:255
  50.5 481.2 %all-gather.56.cloned.1.call-start = ((), (), s32[]{:S(2)}) async-start(), calls=%async_computation.18 | async-start | bytes 1769472 | tf_op jit(solution)/shard_map/all_gather | solution.py:256
  51.3 489.2 %all-gather.44.cloned.1.call-start = ((), (), s32[]{:S(2)}) async-start(), calls=%async_computation.12 | async-start | bytes 5898240 | tf_op jit(solution)/shard_map/all_gather | solution.py:485
  52.0 504.0 %all-gather.46.cloned.1.call-start = ((), (), s32[]{:S(2)}) async-start(), calls=%async_computation.13 | async-start | bytes 5898240 | tf_op jit(solution)/shard_map/all_gather | solution.py:487
  52.6 509.8 %all-gather.48.cloned.1.call-start = ((), (), s32[]{:S(2)}) async-start(), calls=%async_computation.14 | async-start | bytes 1474560 | tf_op jit(solution)/shard_map/all_gather | solution.py:492
  53.4 533.8 %all-gather.54.cloned.1.call-start = ((), (), s32[]{:S(2)}) async-start(), calls=%async_computation.17 | async-start | bytes 17694720 | tf_op jit(solution)/shard_map/all_gather | solution.py:494
  54.0 57.1 %copy-start.427 = (bf16[768]{0:T(1024)(128)(2,1)S(1)}, bf16[768]{0:T(1024)(128)(2,1)}, u32[]{:S(2)}) copy-start(bf16[768]{0:T(1024)(128)(2,1)} %param.49) | copy-start | bytes 4612
  54.0 1141.4 %all-gather.64.cloned.1.call-start = ((), (), s32[]{:S(2)}) async-start(), calls=%async_computation.22 | async-start | bytes 1769472 | tf_op jit(solution)/shard_map/all_gather | solution.py:373
  54.1 71.1 %copy-start.408 = (s32[128]{0:T(128)}, s32[128]{0:T(128)S(1)}, u32[]{:S(2)}) copy-start(s32[128]{0:T(128)S(1)} %get-tuple-element.1764) | copy-start | bytes 1540
  54.1 71.1 %copy-start.410 = (s32[128]{0:T(128)}, s32[128]{0:T(128)S(1)}, u32[]{:S(2)}) copy-start(s32[128]{0:T(128)S(1)} %get-tuple-element.1765) | copy-start | bytes 1540
  54.3 71.0 %copy-start.428 = (s32[128]{0:T(128)}, s32[128]{0:T(128)S(1)}, u32[]{:S(2)}) copy-start(s32[128]{0:T(128)S(1)} %get-tuple-element.1763) | copy-start | bytes 1540
  54.3 71.0 %copy-start.429 = (s32[128]{0:T(128)}, s32[128]{0:T(128)S(1)}, u32[]{:S(2)}) copy-start(s32[128]{0:T(128)S(1)} %get-tuple-element.1762) | copy-start | bytes 1540
  55.1 70.2 %copy-start.92 = (bf16[1,170,768]{2,0,1:T(2,128)(2,1)}, bf16[1,170,768]{2,0,1:T(2,128)(2,1)S(1)}, u32[]{:S(2)}) copy-start(bf16[1,170,768]{2,0,1:T(2,128)(2,1)S(1)} %get-tuple-element.1464) | copy-start | bytes 783364
  55.1 70.2 %copy-start.94 = (bf16[1,170,768]{2,0,1:T(2,128)(2,1)}, bf16[1,170,768]{2,0,1:T(2,128)(2,1)S(1)}, u32[]{:S(2)}) copy-start(bf16[1,170,768]{2,0,1:T(2,128)(2,1)S(1)} %get-tuple-element.1463) | copy-start | bytes 783364
  69.0 57.0 %copy-start.248 = (f32[384]{0:T(512)}, f32[384]{0:T(512)S(1)}, u32[]{:S(2)}) copy-start(f32[384]{0:T(512)S(1)} %get-tuple-element.1748) | copy-start | bytes 4612
  69.0 57.0 %copy-start.250 = (f32[384]{0:T(512)}, f32[384]{0:T(512)S(1)}, u32[]{:S(2)}) copy-start(f32[384]{0:T(512)S(1)} %get-tuple-element.1747) | copy-start | bytes 4612
  127.0 86.0 %copy-start.56 = (f32[170,384]{1,0:T(8,128)}, f32[170,384]{1,0:T(8,128)S(1)}, u32[]{:S(2)}) copy-start(f32[170,384]{1,0:T(8,128)S(1)} %get-tuple-element.1650) | copy-start | bytes 783364
  127.0 146.1 %copy-start.57 = (f32[170,384]{1,0:T(8,128)}, f32[170,384]{1,0:T(8,128)S(1)}, u32[]{:S(2)}) copy-start(f32[170,384]{1,0:T(8,128)S(1)} %get-tuple-element.1651) | copy-start | bytes 783364
  127.0 203.9 %copy-start.53 = (f32[170,384]{1,0:T(8,128)}, f32[170,384]{1,0:T(8,128)S(1)}, u32[]{:S(2)}) copy-start(f32[170,384]{1,0:T(8,128)S(1)} %get-tuple-element.1451) | copy-start | bytes 783364
  127.0 286.5 %copy-start.55 = (f32[170,384]{1,0:T(8,128)}, f32[170,384]{1,0:T(8,128)S(1)}, u32[]{:S(2)}) copy-start(f32[170,384]{1,0:T(8,128)S(1)} %get-tuple-element.1446) | copy-start | bytes 783364
  214.1 57.2 %copy-start.187 = (f32[42,384]{1,0:T(8,128)S(1)}, f32[42,384]{1,0:T(8,128)}, u32[]{:S(2)}) copy-start(f32[42,384]{1,0:T(8,128)} %slice.1962) | copy-start | bytes 193540
  214.1 57.2 %copy-start.188 = (f32[42,384]{1,0:T(8,128)S(1)}, f32[42,384]{1,0:T(8,128)}, u32[]{:S(2)}) copy-start(f32[42,384]{1,0:T(8,128)} %slice.1924) | copy-start | bytes 193540
  331.5 62.4 %copy-start.225 = (f32[10,384]{1,0:T(8,128)S(1)}, f32[10,384]{1,0:T(8,128)}, u32[]{:S(2)}) copy-start(f32[10,384]{1,0:T(8,128)} %slice.2107) | copy-start | bytes 46084
  332.4 76.6 %copy-start.123 = (f32[170,384]{1,0:T(8,128)}, f32[170,384]{1,0:T(8,128)S(1)}, u32[]{:S(2)}) copy-start(f32[170,384]{1,0:T(8,128)S(1)} %pad.780) | copy-start | bytes 783364
  332.5 78.3 %copy-start.125 = (f32[170,384]{1,0:T(8,128)}, f32[170,384]{1,0:T(8,128)S(1)}, u32[]{:S(2)}) copy-start(f32[170,384]{1,0:T(8,128)S(1)} %pad.781) | copy-start | bytes 783364
  414.0 55.5 %copy-start.223 = (f32[384]{0:T(512)S(1)}, f32[384]{0:T(512)}, u32[]{:S(2)}) copy-start(f32[384]{0:T(512)} %custom-call.3) | copy-start | bytes 4612
  415.0 64.3 %copy-start.221 = (f32[384]{0:T(512)S(1)}, f32[384]{0:T(512)}, u32[]{:S(2)}) copy-start(f32[384]{0:T(512)} %custom-call) | copy-start | bytes 4612
  415.1 59.9 %copy-start.137 = (f32[170,384]{1,0:T(8,128)}, f32[170,384]{1,0:T(8,128)S(1)}, u32[]{:S(2)}) copy-start(f32[170,384]{1,0:T(8,128)S(1)} %pad.809) | copy-start | bytes 783364
  415.1 70.3 %copy-start.174 = (f32[84,384]{1,0:T(8,128)S(1)}, f32[84,384]{1,0:T(8,128)}, u32[]{:S(2)}) copy-start(f32[84,384]{1,0:T(8,128)} %slice.2150) | copy-start | bytes 387076
  488.7 708.5 %all-gather.60.cloned.1.call-start = ((), (), s32[]{:S(2)}) async-start(), calls=%async_computation.20 | async-start | bytes 1769472 | tf_op jit(solution)/shard_map/all_gather | solution.py:373
  505.0 774.8 %all-gather.66.cloned.1.call-start = ((), (), s32[]{:S(2)}) async-start(), calls=%async_computation.23 | async-start | bytes 1769472 | tf_op jit(solution)/shard_map/all_gather | solution.py:376
  565.6 21.5 collective-permute-start.1
  566.9 27.7 %collective-permute-start = (bf16[1,1536]{1,0:T(2,128)(2,1)}, bf16[1,1536]{1,0:T(2,128)(2,1)}, u32[]{:S(2)}, u32[]{:S(2)}) collective-permute-start(bf16[1,1536]{1,0:T(2,128)(2,1)} %get-tuple-element.1473), channel_id=1, source_target_pairs={{0,4},{4,8},{8,12},{12,16},{16,20},{20,24},{24,28},{1,5},{5,9},{9,... | collective-permute-start | bytes 9224 | tf_op jit(solution)/shard_map/ppermute | solution.py:41
  574.6 24.4 %collective-permute-start.3 = (bf16[1,1536]{1,0:T(2,128)(2,1)}, bf16[1,1536]{1,0:T(2,128)(2,1)}, u32[]{:S(2)}, u32[]{:S(2)}) collective-permute-start(bf16[1,1536]{1,0:T(2,128)(2,1)} %get-tuple-element.1476), channel_id=1, source_target_pairs={{4,0},{8,4},{12,8},{16,12},{20,16},{24,20},{28,24},{5,1},{9,5},{13... | collective-permute-start | bytes 9224 | tf_op jit(solution)/shard_map/ppermute | solution.py:42
  575.9 24.7 %collective-permute-start.2 = (bf16[1,1536]{1,0:T(2,128)(2,1)}, bf16[1,1536]{1,0:T(2,128)(2,1)}, u32[]{:S(2)}, u32[]{:S(2)}) collective-permute-start(bf16[1,1536]{1,0:T(2,128)(2,1)} %get-tuple-element.1475), channel_id=1, source_target_pairs={{0,4},{4,8},{8,12},{12,16},{16,20},{20,24},{24,28},{1,5},{5,9},{9,... | collective-permute-start | bytes 9224 | tf_op jit(solution)/shard_map/ppermute | solution.py:41
  606.9 15.1 collective-permute-start.5
  608.8 14.9 collective-permute-start.4
  611.4 158.4 %collective-permute-start.7 = (bf16[1,1536]{1,0:T(2,128)(2,1)}, bf16[1,1536]{1,0:T(2,128)(2,1)}, u32[]{:S(2)}, u32[]{:S(2)}) collective-permute-start(bf16[1,1536]{1,0:T(2,128)(2,1)} %get-tuple-element.1470), channel_id=1, source_target_pairs={{0,4},{4,8},{8,12},{12,16},{16,20},{20,24},{24,28},{1,5},{5,9},{9,... | collective-permute-start | bytes 9224 | tf_op jit(solution)/shard_map/ppermute | solution.py:41
  616.5 204.7 %collective-permute-start.6 = (bf16[1,1536]{1,0:T(2,128)(2,1)}, bf16[1,1536]{1,0:T(2,128)(2,1)}, u32[]{:S(2)}, u32[]{:S(2)}) collective-permute-start(bf16[1,1536]{1,0:T(2,128)(2,1)} %get-tuple-element.1469), channel_id=1, source_target_pairs={{4,0},{8,4},{12,8},{16,12},{20,16},{24,20},{28,24},{5,1},{9,5},{13... | collective-permute-start | bytes 9224 | tf_op jit(solution)/shard_map/ppermute | solution.py:42
  867.6 70.1 %copy-start.60 = (f32[128,768]{1,0:T(8,128)}, f32[128,768]{1,0:T(8,128)S(1)}, u32[]{:S(2)}) copy-start(f32[128,768]{1,0:T(8,128)S(1)} %get-tuple-element.1659) | copy-start | bytes 1179652
  867.6 79.7 %copy-start.64 = (f32[128,768]{1,0:T(8,128)}, f32[128,768]{1,0:T(8,128)S(1)}, u32[]{:S(2)}) copy-start(f32[128,768]{1,0:T(8,128)S(1)} %get-tuple-element.1366) | copy-start | bytes 1179652
  881.2 60.7 %copy-start.84 = (bf16[128,3072]{1,0:T(8,128)(2,1)}, bf16[128,3072]{1,0:T(8,128)(2,1)S(1)}, u32[]{:S(2)}) copy-start(bf16[128,3072]{1,0:T(8,128)(2,1)S(1)} %get-tuple-element.1791) | copy-start | bytes 2359300
  881.2 60.7 %copy-start.118 = (f32[85,384]{1,0:T(8,128)}, f32[85,384]{1,0:T(8,128)S(1)}, u32[]{:S(2)}) copy-start(f32[85,384]{1,0:T(8,128)S(1)} %pad_maximum_fusion.67) | copy-start | bytes 391684
  953.5 329.0 %all-gather.62.cloned.1.call-start = ((), (), s32[]{:S(2)}) async-start(), calls=%async_computation.21 | async-start | bytes 1769472 | tf_op jit(solution)/shard_map/all_gather | solution.py:376
  960.5 70.2 %copy-start.383 = (f32[1,1,384]{2,1,0:T(1,128)S(1)}, f32[1,1,384]{2,1,0:T(1,128)}, u32[]{:S(2)}) copy-start(f32[1,1,384]{2,1,0:T(1,128)} %add_bitcast_fusion.7) | copy-start | bytes 4612
  960.5 96.2 %copy-start.164 = (f32[85,384]{1,0:T(8,128)S(1)}, f32[85,384]{1,0:T(8,128)}, u32[]{:S(2)}) copy-start(f32[85,384]{1,0:T(8,128)} %add.2105) | copy-start | bytes 391684
  960.5 123.5 %copy-start.169 = (f32[85,384]{1,0:T(8,128)S(1)}, f32[85,384]{1,0:T(8,128)}, u32[]{:S(2)}) copy-start(f32[85,384]{1,0:T(8,128)} %add.2174) | copy-start | bytes 391684
  960.5 151.2 %copy-start.158 = (bf16[128,12,64]{0,2,1:T(8,128)(2,1)S(1)}, bf16[128,12,64]{0,2,1:T(8,128)(2,1)}, u32[]{:S(2)}) copy-start(bf16[128,12,64]{0,2,1:T(8,128)(2,1)} %copy-done.157) | copy-start | bytes 589828
  960.5 151.2 %copy-start.438 = (f32[128]{0:T(128)S(1)}, f32[128]{0:T(128)}, u32[]{:S(2)}) copy-start(f32[128]{0:T(128)} %copy-done.437) | copy-start | bytes 1540
  974.2 109.2 %copy-start.217 = (f32[384]{0:T(512)S(1)}, f32[384]{0:T(512)}, u32[]{:S(2)}) copy-start(f32[384]{0:T(512)} %get-tuple-element.943) | copy-start | bytes 4612
  974.2 431.7 %reduce-scatter.13.cloned.1.call-start = ((), (), s32[]{:S(2)}) async-start(), calls=%async_computation.24 | async-start | bytes 1474560 | tf_op jit(solution)/shard_map/reduce_scatter | solution.py:521
  1115.0 290.9 %reduce-scatter.19.cloned.1.call-start = ((), (), s32[]{:S(2)}) async-start(), calls=%async_computation.27 | async-start | bytes 1474560 | tf_op jit(solution)/shard_map/reduce_scatter | solution.py:551
  1144.5 261.4 %reduce-scatter.21.cloned.1.call-start = ((), (), s32[]{:S(2)}) async-start(), calls=%async_computation.28 | async-start | bytes 1474560 | tf_op jit(solution)/shard_map/reduce_scatter | solution.py:554
  1150.0 261.4 %reduce-scatter.27.cloned.1.call-start = ((), (), s32[]{:S(2)}) async-start(), calls=%async_computation.31 | async-start | bytes 2949120
  1177.6 235.1 %reduce-scatter.15.cloned.1.call-start = ((), (), s32[]{:S(2)}) async-start(), calls=%async_computation.25 | async-start | bytes 5898240 | tf_op jit(solution)/shard_map/reduce_scatter | solution.py:530
  1184.1 228.6 %reduce-scatter.17.cloned.1.call-start = ((), (), s32[]{:S(2)}) async-start(), calls=%async_computation.26 | async-start | bytes 5898240 | tf_op jit(solution)/shard_map/reduce_scatter | solution.py:536
  1190.5 222.3 %reduce-scatter.25.cloned.1.call-start = ((), (), s32[]{:S(2)}) async-start(), calls=%async_computation.30 | async-start | bytes 4423680
  1323.7 165.6 %reduce-scatter.23.cloned.1.call-start = ((), (), s32[]{:S(2)}) async-start(), calls=%async_computation.29 | async-start | bytes 17694720 | tf_op jit(solution)/shard_map/reduce_scatter | solution.py:557
  (430 other events, 4316.5 us)
Sparse Core Ops, SparseCore 0:
  9.6 33.4 all-gather.35
  44.6 24.2 all-gather.49
  70.5 17.4 all-gather.51
  90.0 44.1 all-gather.39
  136.3 42.6 all-gather.37
  180.4 16.2 all-gather.41
  198.9 44.2 all-gather.57
  245.4 42.8 all-gather.55
  289.9 36.3 all-gather.43
  327.7 37.4 all-gather.45
  366.7 17.4 all-gather.47
  385.6 91.0 all-gather.53
  488.8 40.8 all-gather.63
  531.8 42.9 all-gather.59
  953.7 41.1 all-gather.65
  996.9 43.1 all-gather.61
  1115.1 22.5 reduce-scatter.12
  1144.7 22.5 reduce-scatter.18
  1169.8 25.7 reduce-scatter.20
  1198.7 33.0 reduce-scatter.26
  1234.3 47.8 reduce-scatter.14
  1284.9 47.8 reduce-scatter.16
  1336.0 40.3 reduce-scatter.24
  1382.4 106.8 reduce-scatter.22
where the time goes:
time: 2190 us; the launch traced here: 2170 us
  blocking collectives  1210 us (55%)
  local copies, waits for them, and re-layouts  392 us (18%)
  matrix products  233 us (11%)
  other arithmetic  174 us (8%)
  waiting for transfers between devices  115 us (5%)
  between operations  28.6 us (1%)
  starting transfers between devices  24.2 us (1%)
    psum x1, blocking collectives, local(): lax.psum((shares[0], shares[1], shares[2], shares[3], shares[4], shares[5...  674 us
    all_gather x16, blocking collectives, entering(): pieces = jax.tree.map(lambda part: lax.all_gather(part, axis), value)  417 us
    slice x104, local copies, waits for them, and re-layouts, micro_step(): lax.associative_scan(chain, (fwd_decay[::-1], (fwd_decay * d_fwd)[::-1]))  76.8 us
    reduce_scatter x1, waiting for transfers between devices, local(): lax.psum_scatter(sums[13].astype(jnp.bfloat16), 'fsdp', scatter_dimension...  75 us
    dot_general x20, matrix products, matmul_tn(): lax.dot_general(left, right, (((0,), (0,)), ((), ())), preferred_element_...  63 us
    slice x94, local copies, waits for them, and re-layouts, micro_step(): badj_cum = lax.associative_scan(chain, (bwd_decay, bwd_decay * d_bwd))  62.3 us
    dot_general x20, matrix products, matmul_nt(): lax.dot_general(left, right, (((1,), (1,)), ((), ())), preferred_element_...  52.2 us
    all_gather x2, blocking collectives, micro_step(): lax.all_gather(delta.astype(jnp.bfloat16), 'ctx', axis=0, tiled=True)  52 us
  transfers between devices with their start and end apart: 32, of which 2 were waited for; matrix products, arithmetic and copies ran while one was open for 36% of the time, Pallas kernels for 0%

commit v1 on v0

v1 whole, which is shorter than its diff:
```python
import functools

import jax
import jax.numpy as jnp
from jax import lax
from jax.experimental import pallas as pl
from jax.experimental.pallas import tpu as pltpu
from jax.sharding import PartitionSpec as P

HEADS = 12
HEAD_DIM = 64
GRU_H = 384
EPSILON = 1e-05
BLOCK_LIMIT = 1024
FAR = 1e9
VMEM_BYTES = 40 * 1024 * 1024

F32 = jnp.float32
BF16 = jnp.bfloat16


def matmul(left, right):
    return jnp.dot(left, right, preferred_element_type=F32)


def matmul_nt(left, right):
    return lax.dot_general(left, right, (((1,), (1,)), ((), ())), preferred_element_type=F32)


def matmul_tn(left, right):
    return lax.dot_general(left, right, (((0,), (0,)), ((), ())), preferred_element_type=F32)


def layer_norm(value, gain, shift):
    center = value - jnp.mean(value, axis=-1, keepdims=True)
    inverse = lax.rsqrt(jnp.mean(center * center, axis=-1, keepdims=True) + EPSILON)
    normed = center * inverse
    return normed * gain + shift, (normed, inverse)


def layer_norm_back(grad, gain, kept):
    normed, inverse = kept
    scaled = grad * gain
    into = inverse * (
        scaled
        - jnp.mean(scaled, axis=-1, keepdims=True)
        - normed * jnp.mean(scaled * normed, axis=-1, keepdims=True)
    )
    return into, jnp.sum(grad * normed, axis=0), jnp.sum(grad, axis=0)


def params(**more):
    return pltpu.CompilerParams(vmem_limit_bytes=VMEM_BYTES, **more)


def cost(flops, moved, transcendentals=0):
    return pl.CostEstimate(
        flops=int(flops), bytes_accessed=int(moved), transcendentals=int(transcendentals)
    )


def two_parts(value):
    high = value.astype(BF16)
    return high, (value - high.astype(F32)).astype(BF16)


def shift_rows(value, by, fill, up):
    rows = value.shape[0]
    row = lax.broadcasted_iota(jnp.int32, value.shape, 0)
    if up:
        return jnp.where(row < rows - by, pltpu.roll(value, rows - by, 0), fill)
    return jnp.where(row >= by, pltpu.roll(value, by, 0), fill)


def scan_rows(decay, drive, up):
    by = 1
    while by < decay.shape[0]:
        drive = drive + decay * shift_rows(drive, by, 0.0, up)
        decay = decay * shift_rows(decay, by, 1.0, up)
        by = by * 2
    return decay, drive


def gru_forward_kernel(
    real, chars_ref, w_ref, bias_ref, start_ref, first_ref, end_ref, last_ref,
    gate_ref, cand_ref, decay_ref, cum_ref, state_ref,
):
    columns = matmul(chars_ref[0], w_ref[...])
    rows = columns.shape[0]
    tokens = start_ref.shape[2]
    place = lax.broadcasted_iota(jnp.int32, (rows, tokens), 0)
    inside = lax.broadcasted_iota(jnp.int32, (rows, GRU_H), 0) < real
    resets = [
        jnp.sum(jnp.where(place == at[0], flag[0], 0.0), axis=1, keepdims=True)
        for at, flag in ((start_ref, first_ref), (end_ref, last_ref))
    ]
    for side in (0, 1):
        cols = pl.ds(side * GRU_H, GRU_H)
        base = 2 * side * GRU_H
        gate = jax.nn.sigmoid(columns[:, base : base + GRU_H] + bias_ref[:, cols])
        cand = jnp.tanh(columns[:, base + GRU_H : base + 2 * GRU_H])
        decay = jnp.where(inside, gate * (1.0 - resets[side]), 1.0)
        drive = jnp.where(inside, (1.0 - gate) * cand, 0.0)
        gate_ref[0, :, cols] = gate
        cand_ref[0, :, cols] = cand
        decay_ref[0, :, cols] = decay
        cum, state = scan_rows(decay, drive, side == 1)
        cum_ref[0, :, cols] = cum
        state_ref[0, :, cols] = state


def char_tok_kernel(state_ref, cum_ref, enter_ref, end_ref, start_ref, out_ref):
    state = state_ref[0] + cum_ref[0] * enter_ref[0]
    high, low = two_parts(state)
    tokens = end_ref.shape[1]
    place = lax.broadcasted_iota(jnp.int32, (tokens, state.shape[0]), 1)
    for side, at in ((0, end_ref), (1, start_ref)):
        pick = jnp.where(place == at[0], 1.0, 0.0).astype(BF16)
        cols = slice(side * GRU_H, (side + 1) * GRU_H)
        out_ref[0, :, pl.ds(side * GRU_H, GRU_H)] = matmul(pick, high[:, cols]) + matmul(
            pick, low[:, cols]
        )


def gru_back_kernel(grad_ref, decay_ref, end_ref, start_ref, spread_ref, cum_ref, carried_ref):
    rows = decay_ref.shape[1]
    tokens = end_ref.shape[2]
    place = lax.broadcasted_iota(jnp.int32, (rows, tokens), 0)
    high, low = two_parts(grad_ref[0])
    for side, at in ((0, end_ref), (1, start_ref)):
        put = jnp.where(place == at[0], 1.0, 0.0).astype(BF16)
        cols = slice(side * GRU_H, (side + 1) * GRU_H)
        there = pl.ds(side * GRU_H, GRU_H)
        spread = matmul(put, high[:, cols]) + matmul(put, low[:, cols])
        decay = decay_ref[0, :, there]
        cum, carried = scan_rows(decay, decay * spread, side == 0)
        spread_ref[0, :, there] = spread
        cum_ref[0, :, there] = cum
        carried_ref[0, :, there] = carried


def gru_grad_kernel(
    real, gate_ref, cand_ref, decay_ref, cum_ref, state_ref, enter_ref,
    spread_ref, back_cum_ref, carried_ref, back_enter_ref, out_ref, bias_ref,
):
    rows = gate_ref.shape[1]
    inside = lax.broadcasted_iota(jnp.int32, (rows, GRU_H), 0) < real
    for side in (0, 1):
        there = pl.ds(side * GRU_H, GRU_H)
        gate = gate_ref[0, :, there]
        cand = cand_ref[0, :, there]
        decay = decay_ref[0, :, there]
        enter = enter_ref[0, :, there]
        back_enter = back_enter_ref[0, :, there]
        state = state_ref[0, :, there] + cum_ref[0, :, there] * enter
        carried = carried_ref[0, :, there] + back_cum_ref[0, :, there] * back_enter
        previous = shift_rows(state, 1, enter, side == 1)
        adjoint = spread_ref[0, :, there] + shift_rows(carried, 1, back_enter, side == 0)
        adjoint = jnp.where(inside, adjoint, 0.0)
        rest = adjoint * (1.0 - gate)
        to_gate = rest * (previous * decay - cand * gate)
        to_cand = rest * (1.0 - cand * cand)
        out_ref[0, :, pl.ds(2 * side * GRU_H, GRU_H)] = to_gate.astype(BF16)
        out_ref[0, :, pl.ds((2 * side + 1) * GRU_H, GRU_H)] = to_cand.astype(BF16)
        bias_ref[0, :, there] = jnp.sum(to_gate, axis=0, keepdims=True)


def per_sequence(*tail):
    return pl.BlockSpec((1,) + tail, lambda s: (s,) + (0,) * len(tail))


def whole_block(*shape):
    return pl.BlockSpec(shape, lambda s: (0,) * len(shape))


def gru_forward(chars, w_gru, bias, start, first, end, last, real):
    batch, rows, width = chars.shape
    tokens = start.shape[2]
    two = 2 * GRU_H
    kept = jax.ShapeDtypeStruct((batch, rows, two), F32)
    return pl.pallas_call(
        functools.partial(gru_forward_kernel, real),
        grid=(batch,),
        in_specs=[per_sequence(rows, width), whole_block(width, 2 * two), whole_block(1, two)]
        + [per_sequence(1, tokens)] * 4,
        out_specs=[per_sequence(rows, two)] * 5,
        out_shape=[kept] * 5,
        compiler_params=params(),
        cost_estimate=cost(
            2 * batch * rows * width * 2 * two,
            chars.size * 2 + w_gru.size * 2 + 20 * batch * rows * two,
            2 * batch * rows * two,
        ),
        name="gru_forward",
    )(chars, w_gru, bias, start, first, end, last)


def gather_states(state, cum, enter, end, start):
    batch, rows, two = state.shape
    tokens = end.shape[1]
    return pl.pallas_call(
        char_tok_kernel,
        grid=(batch,),
        in_specs=[per_sequence(rows, two)] * 2
        + [per_sequence(1, two)]
        + [per_sequence(tokens, 1)] * 2,
        out_specs=per_sequence(tokens, two),
        out_shape=jax.ShapeDtypeStruct((batch, tokens, two), F32),
        compiler_params=params(),
        cost_estimate=cost(
            4 * batch * rows * tokens * two, 8 * batch * rows * two + 4 * batch * tokens * two
        ),
        name="gather_states",
    )(state, cum, enter, end, start)


def gru_back(grad, decay, end, start):
    batch, rows, two = decay.shape
    tokens = end.shape[2]
    kept = jax.ShapeDtypeStruct((batch, rows, two), F32)
    return pl.pallas_call(
        gru_back_kernel,
        grid=(batch,),
        in_specs=[per_sequence(tokens, two), per_sequence(rows, two)]
        + [per_sequence(1, tokens)] * 2,
        out_specs=[per_sequence(rows, two)] * 3,
        out_shape=[kept] * 3,
        compiler_params=params(),
        cost_estimate=cost(
            4 * batch * rows * tokens * two, 16 * batch * rows * two + 4 * batch * tokens * two
        ),
        name="gru_back",
    )(grad, decay, end, start)


def gru_grad(gate, cand, decay, cum, state, enter, spread, back_cum, carried, back_enter, real):
    batch, rows, two = decay.shape
    big = per_sequence(rows, two)
    row = per_sequence(1, two)
    return pl.pallas_call(
        functools.partial(gru_grad_kernel, real),
        grid=(batch,),
        in_specs=[big] * 5 + [row] + [big] * 3 + [row],
        out_specs=[per_sequence(rows, 2 * two), row],
        out_shape=[
            jax.ShapeDtypeStruct((batch, rows, 2 * two), BF16),
            jax.ShapeDtypeStruct((batch, 1, two), F32),
        ],
        compiler_params=params(),
        cost_estimate=cost(20 * batch * rows * two, 36 * batch * rows * two),
        name="gru_grad",
    )(gate, cand, decay, cum, state, enter, spread, back_cum, carried, back_enter)


def combine_entering(decays, drives, backward):
    count, mine = lax.axis_size("ctx"), lax.axis_index("ctx")
    if backward:
        decays, drives, mine = decays[::-1], drives[::-1], count - 1 - mine
    if count <= 16:
        total = jnp.zeros_like(drives[0])
        for position in range(count - 1):
            total = jnp.where(
                position < mine, decays[position] * total + drives[position], total
            )
        return total

    def hop(position, total):
        return jnp.where(position < mine, decays[position] * total + drives[position], total)

    return lax.fori_loop(0, count - 1, hop, jnp.zeros_like(drives[0]))


def entering_states(decays, drives, flip):
    left = combine_entering(decays[:, :, :GRU_H], drives[:, :, :GRU_H], flip)
    right = combine_entering(decays[:, :, GRU_H:], drives[:, :, GRU_H:], not flip)
    return jnp.concatenate([left, right], axis=-1)[:, None, :]


def project_kernel(groups, part, tok_ref, w_ref, seg_ref, out_ref):
    qkv = matmul(tok_ref[0], w_ref[...]).astype(BF16)
    rows, width = tok_ref.shape[1], tok_ref.shape[2]
    lane = lax.broadcasted_iota(jnp.int32, (rows, HEAD_DIM), 1)
    marks = jnp.where(lane == seg_ref[0], 1.0, 0.0).astype(BF16)
    for group in range(groups):
        pieces = [
            qkv[:, kind * width + group * part : kind * width + (group + 1) * part]
            for kind in range(3)
        ]
        out_ref[group] = jnp.concatenate(pieces + [marks], axis=1)


def attend_kernel(heads, all_ref, query_ref, edge_ref, out_ref, kept_ref, key_scr, value_scr):
    part = heads * HEAD_DIM
    rows = query_ref.shape[0]

    @pl.when(pl.program_id(0) == 0)
    def build():
        marks = all_ref[:, 3 * part :]
        blocked = ((marks.astype(F32) - 1.0) * FAR).astype(BF16)
        ones = jnp.ones_like(marks)
        for head in range(heads):
            at = head * HEAD_DIM
            key_scr[head] = jnp.concatenate(
                [all_ref[:, part + at : part + at + HEAD_DIM], blocked], axis=1
            )
            value_scr[head] = jnp.concatenate(
                [all_ref[:, 2 * part + at : 2 * part + at + HEAD_DIM], ones], axis=1
            )

    marks = query_ref[:, 3 * part :]
    outs = []
    for head in range(heads):
        at = head * HEAD_DIM
        query = query_ref[:, at : at + HEAD_DIM] * jnp.asarray(HEAD_DIM ** (-0.5), BF16)
        query = jnp.concatenate([query, marks], axis=1)
        expvals = jnp.exp(matmul_nt(query, key_scr[head]))
        both = matmul(expvals.astype(BF16), value_scr[head])
        total = both[:, HEAD_DIM:]
        context = both[:, :HEAD_DIM] / total
        kept_ref[:, pl.ds(head * 2 * HEAD_DIM, 2 * HEAD_DIM)] = jnp.concatenate(
            [context, total], axis=1
        )
        outs.append(context.astype(BF16))
    outs.append(jnp.concatenate([edge_ref[...]] * (rows // edge_ref.shape[0]), axis=0))
    out_ref[...] = jnp.concatenate(outs, axis=1)


def attend_back_kernel(
    heads, all_ref, kept_ref, grad_ref, out_ref, query_scr, key_scr, value_scr, grad_scr
):
    part = heads * HEAD_DIM
    rows = out_ref.shape[0]
    step = pl.program_id(0)

    @pl.when(step == 0)
    def build():
        marks = all_ref[:, 3 * part :]
        blocked = ((marks.astype(F32) - 1.0) * FAR).astype(BF16)
        lane = lax.broadcasted_iota(jnp.int32, marks.shape, 1)
        pair = jnp.where(lane < 2, 1.0, 0.0).astype(BF16)
        for head in range(heads):
            at = head * HEAD_DIM
            query = all_ref[:, at : at + HEAD_DIM] * jnp.asarray(HEAD_DIM ** (-0.5), BF16)
            query_scr[head] = jnp.concatenate([query, marks], axis=1)
            key_scr[head] = jnp.concatenate(
                [all_ref[:, part + at : part + at + HEAD_DIM], blocked], axis=1
            )
            value_scr[head] = jnp.concatenate(
                [all_ref[:, 2 * part + at : 2 * part + at + HEAD_DIM], pair], axis=1
            )
            context = kept_ref[:, 2 * at : 2 * at + HEAD_DIM]
            total = kept_ref[:, 2 * at + HEAD_DIM : 2 * at + 2 * HEAD_DIM]
            grad = grad_ref[:, at : at + HEAD_DIM].astype(F32) / total
            delta = jnp.sum(grad * context, axis=1, keepdims=True)
            high, low = two_parts(-delta)
            extra = jnp.where(
                lane == 0, high.astype(F32), jnp.where(lane == 1, low.astype(F32), 0.0)
            )
            grad_scr[head] = jnp.concatenate([grad, extra], axis=1).astype(BF16)

    here = pl.ds(pl.multiple_of(step * rows, rows), rows)
    scale = HEAD_DIM ** (-0.5)
    d_query, d_key, d_value = [], [], []
    for head in range(heads):
        expvals = jnp.exp(matmul_nt(query_scr[head, here], key_scr[head]))
        inner = matmul_nt(grad_scr[head, here], value_scr[head])
        d_scores = (expvals * inner).astype(BF16)
        d_query.append((matmul(d_scores, key_scr[head])[:, :HEAD_DIM] * scale).astype(BF16))
        expvals = jnp.exp(matmul_nt(key_scr[head, here], query_scr[head]))
        inner = matmul_nt(value_scr[head, here], grad_scr[head])
        d_scores = (expvals * inner).astype(BF16)
        d_key.append(matmul(d_scores, query_scr[head])[:, :HEAD_DIM].astype(BF16))
        d_value.append(
            matmul(expvals.astype(BF16), grad_scr[head])[:, :HEAD_DIM].astype(BF16)
        )
    pad = jnp.zeros((rows, HEAD_DIM), BF16)
    out_ref[...] = jnp.concatenate(d_query + d_key + d_value + [pad], axis=1)


def unpack_kernel(groups, part, kinds, in_ref, out_ref):
    pieces = [
        in_ref[group, :, kind * part : (kind + 1) * part]
        for kind in range(kinds)
        for group in range(groups)
    ]
    out_ref[...] = jnp.concatenate(pieces, axis=1)


def send_grad_kernel(groups, part, grad_ref, w_ref, edge_ref, out_ref):
    d_context = matmul_nt(grad_ref[...], w_ref[...]).astype(BF16)
    for group in range(groups):
        out_ref[group] = jnp.concatenate(
            [d_context[:, group * part : (group + 1) * part], edge_ref[...]], axis=1
        )


def heads_here(batch, count):
    if batch * HEADS % count != 0:
        return 0
    heads = batch * HEADS // count
    if heads > HEADS or HEADS % heads != 0 or heads % 2 == 0:
        return 0
    return heads


def edges_block(pieces, rows):
    flat = jnp.concatenate([half.reshape(-1) for piece in pieces for half in two_parts(piece)])
    block = flat.reshape(-1, HEAD_DIM)
    return jnp.pad(block, ((0, rows - block.shape[0]), (0, 0)))


def edges_from(block, shapes):
    count = block.shape[0]
    flat = block.reshape(count, -1).astype(F32)
    out, at = [], 0
    for shape in shapes:
        size = 1
        for extent in shape:
            size = size * extent
        high = flat[:, at : at + size]
        low = flat[:, at + size : at + 2 * size]
        out.append((high + low).reshape((count,) + shape))
        at = at + 2 * size
    return out


def project_and_pack(tokens, w_qkv, segment, heads):
    batch, rows, width = tokens.shape
    groups, part = HEADS // heads, heads * HEAD_DIM
    wide = 3 * part + HEAD_DIM
    return pl.pallas_call(
        functools.partial(project_kernel, groups, part),
        grid=(batch,),
        in_specs=[
            per_sequence(rows, width),
            whole_block(width, 3 * width),
            per_sequence(rows, 1),
        ],
        out_specs=pl.BlockSpec((groups, rows, wide), lambda s: (s, 0, 0)),
        out_shape=jax.ShapeDtypeStruct((batch * groups, rows, wide), BF16),
        compiler_params=params(),
        cost_estimate=cost(
            6 * batch * rows * width * width,
            tokens.size * 2 + w_qkv.size * 2 + 2 * batch * groups * rows * wide,
        ),
        name="project",
    )(tokens, w_qkv, segment[:, :, None])


def attend(everything, edges, heads):
    length, wide = everything.shape
    block = 256
    part = heads * HEAD_DIM
    out_wide = part + HEAD_DIM
    return pl.pallas_call(
        functools.partial(attend_kernel, heads),
        grid=(length // block,),
        in_specs=[
            pl.BlockSpec((length, wide), lambda i: (0, 0)),
            pl.BlockSpec((block, wide), lambda i: (i, 0)),
            pl.BlockSpec(edges.shape, lambda i: (0, 0)),
        ],
        out_specs=[
            pl.BlockSpec((block, out_wide), lambda i: (i, 0)),
            pl.BlockSpec((block, 2 * part), lambda i: (i, 0)),
        ],
        out_shape=[
            jax.ShapeDtypeStruct((length, out_wide), BF16),
            jax.ShapeDtypeStruct((length, 2 * part), F32),
        ],
        scratch_shapes=[
            pltpu.VMEM((heads, length, 2 * HEAD_DIM), BF16),
            pltpu.VMEM((heads, length, 2 * HEAD_DIM), BF16),
        ],
        compiler_params=params(),
        cost_estimate=cost(
            8 * heads * length * length * HEAD_DIM,
            length * (wide * 2 + out_wide * 2 + 8 * part),
            heads * length * length,
        ),
        name="attend",
    )(everything, everything, edges)


def attend_back(everything, kept, grads, heads):
    length, wide = everything.shape
    block = 256
    part = heads * HEAD_DIM
    scratch = pltpu.VMEM((heads, length, 2 * HEAD_DIM), BF16)
    return pl.pallas_call(
        functools.partial(attend_back_kernel, heads),
        grid=(length // block,),
        in_specs=[
            pl.BlockSpec((length, wide), lambda i: (0, 0)),
            pl.BlockSpec((length, 2 * part), lambda i: (0, 0)),
            pl.BlockSpec((length, part + HEAD_DIM), lambda i: (0, 0)),
        ],
        out_specs=pl.BlockSpec((block, wide), lambda i: (i, 0)),
        out_shape=jax.ShapeDtypeStruct((length, wide), BF16),
        scratch_shapes=[scratch] * 4,
        compiler_params=params(),
        cost_estimate=cost(
            28 * heads * length * length * HEAD_DIM,
            length * (wide * 4 + 8 * part + 2 * part),
            2 * heads * length * length,
        ),
        name="attend_back",
    )(everything, kept, grads)


def unpack(received, heads, kinds, batch):
    count, rows, wide = received.shape
    groups, part = HEADS // heads, heads * HEAD_DIM
    width = kinds * groups * part
    return pl.pallas_call(
        functools.partial(unpack_kernel, groups, part, kinds),
        grid=(batch,),
        in_specs=[pl.BlockSpec((groups, rows, wide), lambda s: (s, 0, 0))],
        out_specs=pl.BlockSpec((rows, width), lambda s: (s, 0)),
        out_shape=jax.ShapeDtypeStruct((batch * rows, width), BF16),
        compiler_params=params(),
        cost_estimate=cost(0, 2 * received.size + 2 * batch * rows * width),
        name="unpack",
    )(received)


def send_grad(d_attn, w_out, edges, heads, batch):
    total, width = d_attn.shape
    rows = total // batch
    groups, part = HEADS // heads, heads * HEAD_DIM
    wide = part + HEAD_DIM
    return pl.pallas_call(
        functools.partial(send_grad_kernel, groups, part),
        grid=(batch,),
        in_specs=[
            pl.BlockSpec((rows, width), lambda s: (s, 0)),
            whole_block(width, width),
            whole_block(rows, HEAD_DIM),
        ],
        out_specs=pl.BlockSpec((groups, rows, wide), lambda s: (s, 0, 0)),
        out_shape=jax.ShapeDtypeStruct((batch * groups, rows, wide), BF16),
        compiler_params=params(),
        cost_estimate=cost(
            2 * total * width * width, 2 * (d_attn.size + w_out.size + total * groups * wide)
        ),
        name="send_grad",
    )(d_attn, w_out, edges)


def block_size(rows):
    size = min(rows, BLOCK_LIMIT)
    while rows % size != 0:
        size = size - 1
    return size


def split_blocks(array, size):
    return array.reshape((array.shape[0] // size, size) + array.shape[1:])


def to_heads(matrix):
    return matrix.reshape(matrix.shape[0], HEADS, HEAD_DIM)


def masked_exp(query_heads, key_heads, query_seg, key_seg):
    scores = jnp.einsum(
        "qhd,khd->hqk", query_heads, key_heads, preferred_element_type=F32
    ) * HEAD_DIM ** (-0.5)
    same = (query_seg[:, None] == key_seg[None, :])[None, :, :]
    return jnp.where(same, jnp.exp(scores), 0.0)


def everyone(rows):
    return lax.all_gather(rows, "ctx", axis=0, tiled=True)


def gathered_attention(qkv, seg_row):
    tok_rows, width = qkv.shape[0], qkv.shape[1] // 3
    query_heads = to_heads(qkv[:, :width])
    pieces = (everyone(qkv[:, width : 2 * width]), everyone(qkv[:, 2 * width :]), everyone(seg_row))
    size = block_size(pieces[0].shape[0])

    def step(acc, item):
        key_block, value_block, seg_block = item
        expvals = masked_exp(query_heads, to_heads(key_block), seg_row, seg_block)
        part_num = jnp.einsum(
            "hqk,khd->qhd", expvals.astype(BF16), to_heads(value_block),
            preferred_element_type=F32,
        )
        return ((acc[0] + part_num, acc[1] + jnp.transpose(jnp.sum(expvals, axis=-1))), None)

    (numer, total), unused = lax.scan(
        step,
        (jnp.zeros((tok_rows, HEADS, HEAD_DIM), F32), jnp.zeros((tok_rows, HEADS), F32)),
        tuple(split_blocks(piece, size) for piece in pieces),
    )
    return numer / total[:, :, None], total


def gathered_attention_back(qkv, seg_row, context, total, d_context):
    tok_rows, width = qkv.shape[0], qkv.shape[1] // 3
    scale = HEAD_DIM ** (-0.5)
    d_context = to_heads(d_context)
    query_rows, key_rows, value_rows = (qkv[:, i * width : (i + 1) * width] for i in range(3))
    grad_heads = (d_context / total[:, :, None]).astype(BF16)
    delta = jnp.sum(d_context * context, axis=-1) / total
    key_heads, value_heads, query_heads = (
        to_heads(key_rows), to_heads(value_rows), to_heads(query_rows)
    )
    zero_heads = jnp.zeros((tok_rows, HEADS, HEAD_DIM), F32)
    seg_all = everyone(seg_row)
    size = block_size(seg_all.shape[0])

    def key_step(acc, item):
        query_block, grad_block, delta_block, seg_block = item
        query_h, grad_h = to_heads(query_block), to_heads(grad_block)
        expvals = masked_exp(query_h, key_heads, seg_block, seg_row)
        dprob = jnp.einsum("qhd,khd->hqk", grad_h, value_heads, preferred_element_type=F32)
        dscore = (expvals * (dprob - jnp.transpose(delta_block)[:, :, None])).astype(BF16)
        dkey = acc[0] + scale * jnp.einsum(
            "hqk,qhd->khd", dscore, query_h, preferred_element_type=F32
        )
        dval = acc[1] + jnp.einsum(
            "hqk,qhd->khd", expvals.astype(BF16), grad_h, preferred_element_type=F32
        )
        return ((dkey, dval), None)

    (dkey, dval), unused = lax.scan(
        key_step,
        (zero_heads, zero_heads),
        tuple(
            split_blocks(piece, size)
            for piece in (
                everyone(query_rows),
                everyone(grad_heads.reshape(tok_rows, width)),
                everyone(delta),
                seg_all,
            )
        ),
    )

    def query_step(acc, item):
        key_block, value_block, seg_block = item
        key_h = to_heads(key_block)
        expvals = masked_exp(query_heads, key_h, seg_row, seg_block)
        dprob = jnp.einsum(
            "qhd,khd->hqk", grad_heads, to_heads(value_block), preferred_element_type=F32
        )
        dscore = (expvals * (dprob - jnp.transpose(delta)[:, :, None])).astype(BF16)
        return (
            acc + scale * jnp.einsum("hqk,khd->qhd", dscore, key_h, preferred_element_type=F32),
            None,
        )

    dquery, unused = lax.scan(
        query_step,
        zero_heads,
        tuple(
            split_blocks(piece, size)
            for piece in (everyone(key_rows), everyone(value_rows), seg_all)
        ),
    )
    return jnp.concatenate(
        [part.reshape(tok_rows, width) for part in (dquery, dkey, dval)], axis=1
    ).astype(BF16)


def neighbours(rows):
    count = lax.axis_size("ctx")
    up = [(i, i + 1) for i in range(count - 1)]
    down = [(j, i) for i, j in up]
    before = lax.ppermute(rows[:, -1], "ctx", up)
    after = lax.ppermute(rows[:, 0], "ctx", down)
    return before[:, None], after[:, None]


def shifted(rows):
    before, after = neighbours(rows)
    later = jnp.concatenate([before, rows[:, :-1]], axis=1)
    earlier = jnp.concatenate([rows[:, 1:], after], axis=1)
    return later, earlier


def sum_over_ctx(value):
    count, me = lax.axis_size("ctx"), lax.axis_index("ctx")
    rows = value.shape[0]
    if count != 8 or rows % (8 * count) != 0:
        return lax.psum(value.astype(F32), "ctx")
    steps = (1, 2, 4)
    piece = value
    for bit in steps:
        mine = (me // bit) % 2
        half = piece.shape[0] // 2
        send = lax.dynamic_slice_in_dim(piece, (1 - mine) * half, half, 0)
        keep = lax.dynamic_slice_in_dim(piece, mine * half, half, 0)
        got = lax.ppermute(send, "ctx", [(i, i ^ bit) for i in range(count)])
        piece = (keep.astype(F32) + got.astype(F32)).astype(BF16)
    for bit in reversed(steps):
        mine = (me // bit) % 2
        half = piece.shape[0]
        got = lax.ppermute(piece, "ctx", [(i, i ^ bit) for i in range(count)])
        both = jnp.zeros((2 * half,) + piece.shape[1:], BF16)
        both = lax.dynamic_update_slice_in_dim(both, piece, mine * half, 0)
        piece = lax.dynamic_update_slice_in_dim(both, got, (1 - mine) * half, 0)
    return piece.astype(F32)


def owned_sum(grads, axis=0):
    share = lax.psum_scatter(grads, "fsdp", scatter_dimension=axis, tiled=True)
    return sum_over_ctx(share.reshape(-1, share.shape[-1]))


def local(
    tokens, chars, segment, char_end, w_qkv, w_out, norm1_gain, norm1_bias, w_up, b_up, w_down,
    norm2_gain, norm2_bias, w_gru, b_gate, w_ftok, w_fchr, w_conv, norm3_gain, norm3_bias,
    norm4_gain, norm4_bias, d_token, d_char,
):
    count, me = lax.axis_size("ctx"), lax.axis_index("ctx")
    shards = lax.axis_size("fsdp")
    batch, rows, width = tokens.shape
    char_rows = chars.shape[1]
    total_rows = batch * rows
    heads = heads_here(batch, count)
    padded_rows = -(-char_rows // 8) * 8

    def gather(weight, axis=0):
        return lax.all_gather(weight, "fsdp", axis=axis, tiled=True)

    vectors = (
        norm1_gain, norm1_bias, norm2_gain, norm2_bias, b_gate, norm3_gain, norm3_bias,
        norm4_gain, norm4_bias, b_up,
    )
    packed = jnp.concatenate(vectors)[None, :]
    packed = lax.all_gather(packed, "fsdp", axis=0, tiled=True).astype(F32)
    share = norm1_gain.shape[0]
    (
        norm1_gain, norm1_bias, norm2_gain, norm2_bias, b_gate, norm3_gain, norm3_bias,
        norm4_gain, norm4_bias,
    ) = (packed[:, i * share : (i + 1) * share].reshape(1, -1) for i in range(9))
    b_up = packed[:, 9 * share :].reshape(1, -1)
    w_qkv = gather(w_qkv)
    w_gru = gather(w_gru)
    w_out = gather(w_out)
    w_up = gather(w_up)
    w_down = gather(w_down)
    w_ftok = gather(w_ftok)
    w_fchr = gather(w_fchr)
    w_conv = gather(w_conv, 1)

    start = jnp.concatenate([jnp.zeros((batch, 1), jnp.int32), char_end[:, :-1] + 1], axis=1)
    change = (segment[:, 1:] != segment[:, :-1]).astype(F32)
    first = jnp.concatenate([jnp.broadcast_to((me == 0).astype(F32), (batch, 1)), change], axis=1)
    last = jnp.concatenate(
        [change, jnp.broadcast_to((me == count - 1).astype(F32), (batch, 1))], axis=1
    )
    chars_pad = jnp.pad(chars, ((0, 0), (0, padded_rows - char_rows), (0, 0)))
    gate, cand, decay, cum, state = gru_forward(
        chars_pad, w_gru, b_gate, start[:, None], first[:, None], char_end[:, None],
        last[:, None], char_rows,
    )
    edge_decay = jnp.concatenate([cum[:, char_rows - 1, :GRU_H], cum[:, 0, GRU_H:]], axis=1)
    edge_state = jnp.concatenate([state[:, char_rows - 1, :GRU_H], state[:, 0, GRU_H:]], axis=1)

    flat_tokens = tokens.reshape(total_rows, width)
    if heads:
        sent = project_and_pack(tokens, w_qkv, segment, heads)
        everything = lax.all_to_all(sent, "ctx", 0, 0, tiled=True)
        everything = everything.reshape(count * rows, -1)
        edges = edges_block((edge_decay, edge_state), rows)
        packed_context, kept = attend(everything, edges, heads)
        received = lax.all_to_all(packed_context.reshape(count, rows, -1), "ctx", 0, 0, tiled=True)
        context_b = unpack(received, heads, 1, batch)
        decays, states = edges_from(
            received[:, :, heads * HEAD_DIM :], ((batch, 2 * GRU_H), (batch, 2 * GRU_H))
        )
    else:
        qkv = matmul(flat_tokens, w_qkv).astype(BF16).reshape(batch, rows, -1)
        results = [gathered_attention(qkv[i], segment[i]) for i in range(batch)]
        context_b = jnp.concatenate([r[0].reshape(rows, width) for r in results]).astype(BF16)
        both = lax.all_gather(jnp.stack([edge_decay, edge_state]), "ctx", axis=0)
        decays, states = both[:, 0], both[:, 1]
    enter = entering_states(decays, states, False)

    attn = matmul(context_b, w_out)
    hidden1, kept1 = layer_norm(flat_tokens.astype(F32) + attn, norm1_gain, norm1_bias)
    hidden1_b = hidden1.astype(BF16)
    pre = matmul(hidden1_b, w_up) + b_up
    inner_b = jax.nn.gelu(pre, approximate=False).astype(BF16)
    ffn = matmul(inner_b, w_down)
    hidden2, kept2 = layer_norm(hidden1 + ffn, norm2_gain, norm2_bias)
    hidden2_b = hidden2.astype(BF16)

    char_tok = gather_states(state, cum, enter, char_end[:, :, None], start[:, :, None])
    char_tok = char_tok.reshape(total_rows, width)
    char_tok_b = char_tok.astype(BF16)
    joined = jnp.concatenate(
        [matmul(hidden2_b, w_ftok), matmul(char_tok_b, w_fchr)], axis=1
    ).astype(BF16)

    two = 2 * width
    later, earlier = shifted(joined.reshape(batch, rows, two))
    taps = (later.reshape(total_rows, two), joined, earlier.reshape(total_rows, two))
    conv = matmul(taps[1], w_conv[1]) + matmul(taps[0], w_conv[0]) + matmul(taps[2], w_conv[2])
    token_out, kept3 = layer_norm(hidden2 + conv[:, :width], norm3_gain, norm3_bias)
    char_out, kept4 = layer_norm(char_tok + conv[:, width:], norm4_gain, norm4_bias)

    d_in3, gain3_grad, bias3_grad = layer_norm_back(
        d_token.reshape(total_rows, width).astype(F32), norm3_gain, kept3
    )
    d_in4, gain4_grad, bias4_grad = layer_norm_back(
        d_char.reshape(total_rows, width).astype(F32), norm4_gain, kept4
    )
    d_conv = jnp.concatenate([d_in3, d_in4], axis=1).astype(BF16)
    d_later, d_earlier = shifted(d_conv.reshape(batch, rows, two))
    d_joined = (
        matmul_nt(d_conv, w_conv[1])
        + matmul_nt(d_earlier.reshape(total_rows, two), w_conv[0])
        + matmul_nt(d_later.reshape(total_rows, two), w_conv[2])
    ).astype(BF16)
    conv_grad = jnp.stack([matmul_tn(tap, d_conv).astype(BF16) for tap in taps])
    conv_sum = owned_sum(conv_grad, 1)

    d_tok_part, d_chr_part = d_joined[:, :width], d_joined[:, width:]
    d_hidden2 = d_in3 + matmul_nt(d_tok_part, w_ftok)
    d_char_tok = d_in4 + matmul_nt(d_chr_part, w_fchr)
    ftok_grad = matmul_tn(hidden2_b, d_tok_part).astype(BF16)
    fchr_grad = matmul_tn(char_tok_b, d_chr_part).astype(BF16)

    end_line, start_line = char_end[:, None], start[:, None]
    spread, back_cum, carried = gru_back(
        d_char_tok.reshape(batch, rows, width), decay, end_line, start_line
    )
    edge_carried = jnp.concatenate(
        [carried[:, 0, :GRU_H], carried[:, char_rows - 1, GRU_H:]], axis=1
    )

    d_in2, gain2_grad, bias2_grad = layer_norm_back(d_hidden2, norm2_gain, kept2)
    d_ffn = d_in2.astype(BF16)
    down_grad = matmul_tn(inner_b, d_ffn).astype(BF16)
    second_sum = owned_sum(
        jnp.concatenate(
            [
                down_grad.reshape(shards, -1, width),
                ftok_grad.reshape(shards, -1, width),
                fchr_grad.reshape(shards, -1, width),
            ],
            axis=1,
        ).reshape(-1, width)
    )
    cdf = (1.0 + lax.erf(pre * (0.5**0.5))) * 0.5
    slope = cdf + pre * jnp.exp(-0.5 * pre * pre) * (0.5 / jnp.pi) ** 0.5
    d_pre = matmul_nt(d_ffn, w_down) * slope
    bup_grad = jnp.sum(d_pre, axis=0)
    d_pre_low = d_pre.astype(BF16)
    up_grad = matmul_tn(hidden1_b, d_pre_low).astype(BF16)
    d_hidden1 = d_in2 + matmul_nt(d_pre_low, w_up)
    d_in1, gain1_grad, bias1_grad = layer_norm_back(d_hidden1, norm1_gain, kept1)
    d_attn = d_in1.astype(BF16)
    wout_grad = matmul_tn(context_b, d_attn).astype(BF16)
    third_sum = owned_sum(jnp.concatenate([up_grad, wout_grad], axis=1))

    if heads:
        edges = edges_block((edge_carried,), rows)
        sent = send_grad(d_attn, w_out, edges, heads, batch)
        received = lax.all_to_all(sent, "ctx", 0, 0, tiled=True)
        (carries,) = edges_from(received[:, :, heads * HEAD_DIM :], ((batch, 2 * GRU_H),))
        packed_grad = attend_back(everything, kept, received.reshape(count * rows, -1), heads)
        returned = lax.all_to_all(packed_grad.reshape(count, rows, -1), "ctx", 0, 0, tiled=True)
        d_qkv = unpack(returned, heads, 3, batch)
    else:
        carries = lax.all_gather(edge_carried, "ctx", axis=0)
        d_context = matmul_nt(d_attn, w_out).reshape(batch, rows, width)
        d_qkv = jnp.concatenate(
            [
                gathered_attention_back(
                    qkv[i], segment[i], results[i][0], results[i][1], d_context[i]
                )
                for i in range(batch)
            ]
        )
    back_enter = entering_states(decays, carries, True)
    d_gate_in, bgate_grad = gru_grad(
        gate, cand, decay, cum, state, enter, spread, back_cum, carried, back_enter, char_rows
    )
    d_gate_in = d_gate_in.reshape(batch * padded_rows, -1)
    gru_weight_grad = matmul_tn(chars_pad.reshape(batch * padded_rows, width), d_gate_in)
    d_chars = matmul_nt(d_gate_in, w_gru).astype(BF16)
    d_chars = d_chars.reshape(batch, padded_rows, width)[:, :char_rows]

    qkv_grad = matmul_tn(flat_tokens, d_qkv).astype(BF16)
    d_tokens = (d_in1 + matmul_nt(d_qkv, w_qkv)).astype(BF16)

    small = jnp.stack(
        [
            gain1_grad, bias1_grad, gain2_grad, bias2_grad, jnp.sum(bgate_grad, axis=(0, 1)),
            gain3_grad, bias3_grad, gain4_grad, bias4_grad,
        ],
        axis=1,
    )
    up_small = bup_grad.reshape(shards, -1, width // shards)
    up_small = jnp.swapaxes(up_small, 1, 2).reshape(width, -1)
    small = jnp.concatenate([small, up_small], axis=1)
    small_count = small.shape[1]
    small = jnp.pad(small, ((0, 0), (0, 128 - small_count)))
    fourth_sum = owned_sum(
        jnp.concatenate([qkv_grad, gru_weight_grad.astype(BF16), small.astype(BF16)], axis=1)
    )

    wide_up, wide_qkv, wide_gru = w_up.shape[1], w_qkv.shape[1], w_gru.shape[1]
    own = width // shards
    own_down = w_down.shape[0] // shards
    vector = fourth_sum[:, wide_qkv + wide_gru :]
    return (
        token_out.astype(BF16).reshape(batch, rows, width),
        char_out.astype(BF16).reshape(batch, rows, width),
        d_tokens.reshape(batch, rows, width),
        d_chars,
        fourth_sum[:, :wide_qkv],
        third_sum[:, wide_up:],
        vector[:, 0],
        vector[:, 1],
        third_sum[:, :wide_up],
        jnp.swapaxes(vector[:, 9:small_count], 0, 1).reshape(-1),
        second_sum[:own_down],
        vector[:, 2],
        vector[:, 3],
        fourth_sum[:, wide_qkv : wide_qkv + wide_gru],
        vector[:, 4],
        second_sum[own_down : own_down + own],
        second_sum[own_down + own :],
        conv_sum.reshape(w_conv.shape[0], -1, two),
        vector[:, 5],
        vector[:, 6],
        vector[:, 7],
        vector[:, 8],
    )


def solution(mesh):
    rows = P("fsdp", "ctx", None)
    pairs = P("fsdp", "ctx")
    matrix = P("fsdp", None)
    vector = P("fsdp")
    weights = (
        matrix, matrix, vector, vector, matrix, vector, matrix, vector, vector, matrix, vector,
        matrix, matrix, P(None, "fsdp", None), vector, vector, vector, vector,
    )
    return jax.shard_map(
        local,
        mesh=mesh,
        in_specs=(rows, rows, pairs, pairs) + weights + (rows, rows),
        out_specs=(rows,) * 4 + weights,
        check_vma=False,
    )
```

time: 2190 us -> 836 us (0.38)
  blocking collectives: 1210 us -> 31.2 us
  waiting for transfers between devices: 115 us -> 491 us
  local copies, waits for them, and re-layouts: 392 us -> 88.4 us
  matrix products: 233 us -> 66 us
  other arithmetic: 174 us -> 49 us
  Pallas kernels: 0 us -> 31.8 us
  starting transfers between devices: 24.2 us -> 53 us
    psum x1 -> x0, blocking collectives: 674 us -> none  [local(): lax.psum((shares[0], shares[1], shares[2], shares[3], shares[4], shares[5...]
    all_gather x21 -> x0, blocking collectives: 511 us -> none  [the longest x16 417 us: entering(): pieces = jax.tree.map(lambda part: lax.all_gather(part, axis), value)]
    slice x420 -> x12, local copies, waits for them, and re-layouts: 242 us -> 10.8 us  [the longest x1 2.87 us: local(): vector[:, 8]]
    ppermute x8 -> x28, waiting for transfers between devices: 0.02 us -> 230 us  [the longest x12 131 us: sum_over_ctx(): got = lax.ppermute(send, 'ctx', [(i, i ^ bit) for i in range(count)])]
    all_gather x16 -> x8, waiting for transfers between devices: 33.7 us -> 175 us  [gather(): return lax.all_gather(weight, 'fsdp', axis=axis, tiled=True)]
    dot_general x32 -> x8, matrix products: 118 us -> 31.5 us  [matmul(): return jnp.dot(left, right, preferred_element_type=F32)]
    pad x188 -> x1, local copies, waits for them, and re-layouts: 46.8 us -> 0.04 us  [local(): chars_pad = jnp.pad(chars, ((0, 0), (0, padded_rows - char_rows), (0, 0)))]
    dot_general x20 -> x10, matrix products: 63 us -> 16.6 us  [matmul_tn(): lax.dot_general(left, right, (((0,), (0,)), ((), ())), preferred_element_...]
  transfers between devices with their start and end apart: 32 -> 43, of which waited for: 2 -> 28; matrix products, arithmetic and copies ran while one was open for 36% -> 17% of each run, Pallas kernels for 0% -> 4%
where the time goes in v1:
time: 836 us; the launch traced here: 828 us
  waiting for transfers between devices  491 us (59%)
  local copies, waits for them, and re-layouts  88.4 us (11%)
  matrix products  66 us (8%)
  starting transfers between devices  53 us (6%)
  other arithmetic  49 us (6%)
  Pallas kernels  31.8 us (4%)
  blocking collectives  31.2 us (4%)
  between operations  17.3 us (2%)
    all_gather x8, waiting for transfers between devices, gather(): return lax.all_gather(weight, 'fsdp', axis=axis, tiled=True)  175 us
    ppermute x12, waiting for transfers between devices, sum_over_ctx(): got = lax.ppermute(send, 'ctx', [(i, i ^ bit) for i in range(count)])  131 us
    ppermute x12, waiting for transfers between devices, sum_over_ctx(): got = lax.ppermute(piece, 'ctx', [(i, i ^ bit) for i in range(count)])  96 us
    reduce_scatter x4, waiting for transfers between devices, owned_sum(): share = lax.psum_scatter(grads, 'fsdp', scatter_dimension=axis, tiled=True)  69 us
    unnamed x217, local copies, waits for them, and re-layouts  41.7 us
    dot_general x8, matrix products, matmul(): return jnp.dot(left, right, preferred_element_type=F32)  31.5 us
    ppermute x12, starting transfers between devices, sum_over_ctx(): got = lax.ppermute(send, 'ctx', [(i, i ^ bit) for i in range(count)])  20.7 us
    all_to_all x1, blocking collectives, local(): received = lax.all_to_all(sent, 'ctx', 0, 0, tiled=True)  19.7 us
  transfers between devices with their start and end apart: 43, of which 28 were waited for; matrix products, arithmetic and copies ran while one was open for 17% of the time, Pallas kernels for 4%

profile of v1, /device:TPU:0, one launch (start us, length us, event | category | flops | bytes accessed | tf_op | source)
XLA Modules:
  0.0 827.8 jit_solution(3950659660312754740)
XLA Ops:
  12.8 30.3 %all-gather.10.cloned.1.call-done.w_ref = bf16[768,2304]{1,0:T(8,128)(2,1)} async-done(((bf16[192,2304]{1,0:T(8,128)(2,1)}), bf16[768,2304]{1,0:T(8,128)(2,1)}) %all-gather.10.cloned.1.call-update) | async-done | bytes 3538960 | tf_op jit(solution)/shard_map/all_gather | solution.py:727
  43.1 2.0 copy-done.10
  45.1 2.3 project.1
  47.5 5.7 all-to-all-start
  55.8 11.5 %all-reduce.7 = bf16[9984]{0:T(1024)(128)(2,1)S(1)} all-reduce(bf16[9984]{0:T(1024)(128)(2,1)S(1)} %dynamic-update-slice), channel_id=2, replica_groups=mesh['ctx'=8,'fsdp'=4] {'fsdp'}, use_global_device_ids=true, to_apply=%add.7 | all-reduce | flops 9984 | bytes 39936
  70.9 2.5 gru_forward.1
  80.0 5.0 all-to-all-done
  85.0 6.2 attend.1
  93.2 3.6 all-to-all-start.1
  104.6 6.9 all-to-all-done.1.in_ref
  117.9 2.0 fusion.145
  121.0 6.2 all-gather.16.cloned.1.call-done
  127.2 11.3 %fusion.14 = (bf16[256,3072]{1,0:T(8,128)(2,1)}, f32[256,3072]{1,0:T(8,128)}) fusion(f32[3072]{0:T(1024)S(1)} %copy-done.79, bf16[768,3072]{1,0:T(8,128)(2,1)} %all-gather.16.cloned.1.call-done, f32[256,768]{1,0:T(8,128)} %copy-done.35, f32[768]{0:T(1024)S(1)} %add.395, f32[768]{0:T(1024)S(1)} %mul.397, f32[256]{0:T(256)S(1)} %add_rsqrt_fusion.3, ...), kind=kOutput, calls=%fused_computation.33 | convolution fusion | flops 1260847104 | bytes 10244096 | tf_op jit(solution)/shard_map/dot_general | solution.py:23
  138.5 27.6 %all-gather.18.cloned.1.call-done = bf16[3072,768]{1,0:T(8,128)(2,1)} async-done(((bf16[768,768]{1,0:T(8,128)(2,1)}), bf16[3072,768]{1,0:T(8,128)(2,1)}) %all-gather.18.cloned.1.call-update) | async-done | bytes 4718608 | tf_op jit(solution)/shard_map/all_gather | solution.py:727
  166.1 4.5 fusion.146
  172.5 12.5 %all-gather.22.cloned.1.call-done = bf16[768,768]{1,0:T(8,128)(2,1)} async-done(((bf16[192,768]{1,0:T(8,128)(2,1)}), bf16[768,768]{1,0:T(8,128)(2,1)}) %all-gather.22.cloned.1.call-update) | async-done | bytes 1179664 | tf_op jit(solution)/shard_map/all_gather | solution.py:727
  186.9 17.2 %all-gather.20.cloned.1.call-done = bf16[768,768]{1,0:T(8,128)(2,1)} async-done(((bf16[192,768]{1,0:T(8,128)(2,1)}), bf16[768,768]{1,0:T(8,128)(2,1)}) %all-gather.20.cloned.1.call-update) | async-done | bytes 1179664 | tf_op jit(solution)/shard_map/all_gather | solution.py:727
  204.1 2.1 convolution_convert_fusion.11
  206.2 3.4 collective-permute-start
  211.4 3.8 collective-permute-done.1
  217.2 79.5 %all-gather.24.cloned.1.call-done = bf16[3,1536,1536]{2,1,0:T(8,128)(2,1)} async-done(((bf16[3,384,1536]{2,1,0:T(8,128)(2,1)}), bf16[3,1536,1536]{2,1,0:T(8,128)(2,1)}) %all-gather.24.cloned.1.call-update) | async-done | bytes 14155792 | tf_op jit(solution)/shard_map/all_gather | solution.py:727
  296.7 4.0 fusion.7
  300.7 4.5 fusion.28
  313.8 5.0 collective-permute-start.3
  325.9 2.9 fusion.147
  330.5 2.3 multiply_reduce_fusion.1
  335.2 2.9 pad_maximum_fusion.2
  343.9 3.5 pad_maximum_fusion.1
  347.5 2.8 convolution_add_fusion.1
  356.5 19.7 %all_to_all.20 = bf16[8,128,256]{2,1,0:T(8,128)(2,1)S(1)} all-to-all(bf16[8,128,256]{2,1,0:T(8,128)(2,1)S(1)} %send_grad.1), channel_id=1, replica_groups=mesh['ctx'=8,'fsdp'=4] {'ctx'}, dimensions={0} | all-to-all | bytes 1048576 | tf_op jit(solution)/shard_map/all_to_all | solution.py:865
  376.2 15.6 %attend_back.1 = bf16[1024,640]{1,0:T(8,128)(2,1)S(1)} custom-call(bf16[1024,640]{1,0:T(8,128)(2,1)} %bitcast.2.all_ref.query_ref, f32[1024,384]{1,0:T(8,128)S(1)} %copy-done.31, bf16[1024,256]{1,0:T(8,128)(2,1)S(1)} %bitcast.454), custom_call_target="tpu_custom_call" | custom-call | flops 5637144576 | bytes 4587520 | tf_op jit(solution)/shard_map/attend_back/pallas_call | solution.py:490
  392.8 3.8 all-to-all-start.3
  406.0 2.0 slice_convert_fusion
  408.0 2.0 reshape.362
  424.6 4.3 bitcast_convert_fusion
  430.9 3.1 fusion.4
  434.0 8.7 %copy.176 = bf16[768,3968]{1,0:T(8,128)(2,1)} copy(bf16[768,3968]{0,1:T(8,128)(2,1)} %fusion.4) | data formatting | bytes 12189696
  448.4 6.7 pad_maximum_fusion
  455.1 2.2 constant_dynamic-slice_fusion.8
  459.2 15.9 %collective-permute-done.10 = bf16[96,3840]{1,0:T(8,128)(2,1)} collective-permute-done((bf16[96,3840]{1,0:T(8,128)(2,1)}, bf16[96,3840]{1,0:T(8,128)(2,1)}, u32[]{:S(2)}, u32[]{:S(2)}) %collective-permute-start.10) | collective-permute-done | bytes 737312 | tf_op jit(solution)/shard_map/ppermute | solution.py:696
  479.9 7.7 collective-permute-done.11
  488.9 2.2 collective-permute-start.12
  491.1 2.4 convolution_convert_fusion.9
  494.7 3.4 collective-permute-done.12
  500.1 8.0 collective-permute-done.13
  511.0 7.5 collective-permute-done.14
  519.8 12.4 %collective-permute-done.16 = bf16[576,768]{1,0:T(8,128)(2,1)S(1)} collective-permute-done((bf16[576,768]{1,0:T(8,128)(2,1)S(1)}, bf16[576,768]{1,0:T(8,128)(2,1)S(1)}, u32[]{:S(2)}, u32[]{:S(2)}) %collective-permute-start.16) | collective-permute-done | bytes 884768 | tf_op jit(solution)/shard_map/ppermute | solution.py:696
  532.5 2.1 collective-permute-start.17
  534.7 7.8 collective-permute-done.17
  544.6 2.1 constant_dynamic-slice_fusion.11
  547.7 5.1 collective-permute-done.18
  556.9 7.4 collective-permute-done.19
  564.4 69.0 %reduce-scatter.11.cloned.1.call-done = bf16[3,384,1536]{2,1,0:T(8,128)(2,1)} async-done(((bf16[3,1536,1536]{2,1,0:T(8,128)(2,1)}), bf16[3,384,1536]{2,1,0:T(8,128)(2,1)}) %reduce-scatter.11.cloned.1.call-update) | async-done | bytes 3538960 | tf_op jit(solution)/shard_map/reduce_scatter | solution.py:709
  640.5 36.1 %collective-permute-done.22 = bf16[576,1536]{1,0:T(8,128)(2,1)S(1)} collective-permute-done((bf16[576,1536]{1,0:T(8,128)(2,1)S(1)}, bf16[576,1536]{1,0:T(8,128)(2,1)S(1)}, u32[]{:S(2)}, u32[]{:S(2)}) %collective-permute-start.22) | collective-permute-done | bytes 1769504 | tf_op jit(solution)/shard_map/ppermute | solution.py:696
  678.8 2.5 collective-permute-start.6
  681.3 19.4 %collective-permute-done.23 = bf16[288,1536]{1,0:T(8,128)(2,1)S(1)} collective-permute-done((bf16[288,1536]{1,0:T(8,128)(2,1)S(1)}, bf16[288,1536]{1,0:T(8,128)(2,1)S(1)}, u32[]{:S(2)}, u32[]{:S(2)}) %collective-permute-start.23) | collective-permute-done | bytes 884768 | tf_op jit(solution)/shard_map/ppermute | solution.py:696
  704.1 23.0 %collective-permute-done.24 = bf16[144,1536]{1,0:T(8,128)(2,1)S(1)} collective-permute-done((bf16[144,1536]{1,0:T(8,128)(2,1)S(1)}, bf16[144,1536]{1,0:T(8,128)(2,1)S(1)}, u32[]{:S(2)}, u32[]{:S(2)}) %collective-permute-start.24) | collective-permute-done | bytes 442400 | tf_op jit(solution)/shard_map/ppermute | solution.py:696
  727.3 13.3 %collective-permute-done.7 = bf16[24,3968]{1,0:T(8,128)(2,1)S(1)} collective-permute-done((bf16[24,3968]{1,0:T(8,128)(2,1)S(1)}, bf16[24,3968]{1,0:T(8,128)(2,1)S(1)}, u32[]{:S(2)}, u32[]{:S(2)}) %collective-permute-start.7) | collective-permute-done | bytes 190496 | tf_op jit(solution)/shard_map/ppermute | solution.py:701
  740.7 8.0 collective-permute-done.25
  750.6 6.2 collective-permute-done.8
  758.6 17.1 %collective-permute-done.26 = bf16[288,1536]{1,0:T(8,128)(2,1)S(1)} collective-permute-done((bf16[288,1536]{1,0:T(8,128)(2,1)S(1)}, bf16[288,1536]{1,0:T(8,128)(2,1)S(1)}, u32[]{:S(2)}, u32[]{:S(2)}) %collective-permute-start.26) | collective-permute-done | bytes 884768 | tf_op jit(solution)/shard_map/ppermute | solution.py:701
  784.7 2.9 slice_reduce_fusion
  788.0 28.4 %collective-permute-done.27 = bf16[576,1536]{1,0:T(8,128)(2,1)S(1)} collective-permute-done((bf16[576,1536]{1,0:T(8,128)(2,1)S(1)}, bf16[576,1536]{1,0:T(8,128)(2,1)S(1)}, u32[]{:S(2)}, u32[]{:S(2)}) %collective-permute-start.27) | collective-permute-done | bytes 1769504 | tf_op jit(solution)/shard_map/ppermute | solution.py:701
  816.6 3.9 convert.85
  (481 shorter events, 154.9 us)
Async XLA Ops:
  7.2 35.9 %all-gather.10.cloned.1.call-start = ((), (), s32[]{:S(2)}) async-start(), calls=%async_computation.8 | async-start | bytes 4423680 | tf_op jit(solution)/shard_map/all_gather | solution.py:727
  7.9 61.4 %all-gather.12.cloned.1.call-start = ((), (), s32[]{:S(2)}) async-start(), calls=%async_computation.9 | async-start | bytes 2949120 | tf_op jit(solution)/shard_map/all_gather | solution.py:727
  8.7 109.2 %all-gather.14.cloned.1.call-start = ((), (), s32[]{:S(2)}) async-start(), calls=%async_computation.10 | async-start | bytes 1474560 | tf_op jit(solution)/shard_map/all_gather | solution.py:727
  9.4 33.7 %copy-start.6 = (bf16[2,128,768]{2,1,0:T(8,128)(2,1)S(1)}, bf16[2,128,768]{2,1,0:T(8,128)(2,1)}, u32[]{:S(2)}) copy-start(bf16[2,128,768]{2,1,0:T(8,128)(2,1)} %tok_ref.1) | copy-start | bytes 1179652
  9.4 117.8 %all-gather.16.cloned.1.call-start = ((), (), s32[]{:S(2)}) async-start(), calls=%async_computation.11 | async-start | bytes 5898240 | tf_op jit(solution)/shard_map/all_gather | solution.py:727
  10.0 156.1 %all-gather.18.cloned.1.call-start = ((), (), s32[]{:S(2)}) async-start(), calls=%async_computation.12 | async-start | bytes 5898240 | tf_op jit(solution)/shard_map/all_gather | solution.py:727
  10.6 174.4 %all-gather.22.cloned.1.call-start = ((), (), s32[]{:S(2)}) async-start(), calls=%async_computation.14 | async-start | bytes 1474560 | tf_op jit(solution)/shard_map/all_gather | solution.py:727
  11.2 192.9 %all-gather.20.cloned.1.call-start = ((), (), s32[]{:S(2)}) async-start(), calls=%async_computation.13 | async-start | bytes 1474560 | tf_op jit(solution)/shard_map/all_gather | solution.py:727
  11.9 284.8 %all-gather.24.cloned.1.call-start = ((), (), s32[]{:S(2)}) async-start(), calls=%async_computation.15 | async-start | bytes 17694720 | tf_op jit(solution)/shard_map/all_gather | solution.py:727
  45.1 8.0 copy-start.65
  47.4 8.0 copy-start.89
  47.4 7.9 copy-start.90
  47.4 20.1 %copy-start.26 = (s32[2,128]{1,0:T(2,128)S(1)}, s32[2,128]{1,0:T(2,128)}, u32[]{:S(2)}) copy-start(s32[2,128]{1,0:T(2,128)} %param.27) | copy-start | bytes 3076
  47.5 37.6 %all-to-all-start = ((bf16[8,128,640]{2,1,0:T(8,128)(2,1)}), bf16[8,128,640]{2,1,0:T(8,128)(2,1)}, u32[]{:S(2)}, u32[]{:S(2)}) async-start(bf16[8,128,640]{2,1,0:T(8,128)(2,1)} %project.1), calls=%async_computation | async-start | bytes 2621440 | tf_op jit(solution)/shard_map/all_to_all | solution.py:767
  93.2 18.3 %all-to-all-start.1 = ((bf16[8,128,256]{2,1,0:T(8,128)(2,1)}), bf16[8,128,256]{2,1,0:T(8,128)(2,1)S(1)}, u32[]{:S(2)}, u32[]{:S(2)}) async-start(bf16[8,128,256]{2,1,0:T(8,128)(2,1)} %bitcast.455), calls=%async_computation.1 | async-start | bytes 1048576 | tf_op jit(solution)/shard_map/all_to_all | solution.py:771
  96.9 358.3 %reduce-scatter.7.cloned.1.call-start = ((), (), s32[]{:S(2)}) async-start(), calls=%async_computation.16 | async-start | bytes 7372800 | tf_op jit(solution)/shard_map/reduce_scatter | solution.py:709
  99.8 15.5 %copy-start.66 = (f32[768]{0:T(1024)}, f32[768]{0:T(1024)S(1)}, u32[]{:S(2)}) copy-start(f32[768]{0:T(1024)S(1)} %mul.426) | copy-start | bytes 9220
  117.9 9.3 %copy-start.79 = (f32[3072]{0:T(1024)S(1)}, f32[3072]{0:T(1024)}, u32[]{:S(2)}) copy-start(f32[3072]{0:T(1024)} %add.398) | copy-start | bytes 36868
  170.6 33.5 %copy-start.68 = (f32[768]{0:T(1024)S(1)}, f32[768]{0:T(1024)}, u32[]{:S(2)}) copy-start(f32[768]{0:T(1024)} %add.403) | copy-start | bytes 9220
  186.9 109.8 %copy-start.50 = (bf16[256,768]{1,0:T(8,128)(2,1)}, bf16[256,768]{1,0:T(8,128)(2,1)S(1)}, u32[]{:S(2)}) copy-start(bf16[256,768]{1,0:T(8,128)(2,1)S(1)} %convolution_convert_fusion.10) | copy-start | bytes 1179652
  206.2 10.1 %copy-start.60 = (bf16[256,768]{1,0:T(8,128)(2,1)}, bf16[256,768]{1,0:T(8,128)(2,1)S(1)}, u32[]{:S(2)}) copy-start(bf16[256,768]{1,0:T(8,128)(2,1)S(1)} %convolution_convert_fusion.11) | copy-start | bytes 1179652
  206.2 5.1 collective-permute-start
  209.6 5.5 collective-permute-start.1
  296.7 8.6 %copy-start.96 = (bf16[3,1536,1536]{2,1,0:T(8,128)(2,1)S(1)}, bf16[3,1536,1536]{2,1,0:T(8,128)(2,1)}, u32[]{:S(2)}) copy-start(bf16[3,1536,1536]{2,1,0:T(8,128)(2,1)} %all-gather.24.cloned.1.call-done) | copy-start | bytes 42467332
  311.0 9.5 %copy-start.37 = (bf16[256,768]{1,0:T(8,128)(2,1)}, bf16[256,768]{1,0:T(8,128)(2,1)S(1)}, u32[]{:S(2)}) copy-start(bf16[256,768]{1,0:T(8,128)(2,1)S(1)} %get-tuple-element.79) | copy-start | bytes 1179652
  312.4 8.1 copy-start.39
  312.4 7.9 collective-permute-start.2
  313.8 6.7 collective-permute-start.3
  338.1 170.1 %reduce-scatter.9.cloned.1.call-start = ((), (), s32[]{:S(2)}) async-start(), calls=%async_computation.17 | async-start | bytes 8847360 | tf_op jit(solution)/shard_map/reduce_scatter | solution.py:709
  355.3 20.9 %copy-start.31 = (f32[1024,384]{1,0:T(8,128)S(1)}, f32[1024,384]{1,0:T(8,128)}, u32[]{:S(2)}) copy-start(f32[1024,384]{1,0:T(8,128)} %copy-done.30) | copy-start | bytes 4718596
  376.2 15.6 %copy-start.15 = (bf16[8,128,256]{2,1,0:T(8,128)(2,1)}, bf16[8,128,256]{2,1,0:T(8,128)(2,1)S(1)}, u32[]{:S(2)}) copy-start(bf16[8,128,256]{2,1,0:T(8,128)(2,1)S(1)} %all_to_all.20) | copy-start | bytes 1572868
  392.8 8.0 copy-start.82
  392.8 11.1 %copy-start.83 = (bf16[768]{0:T(1024)(128)(2,1)S(1)}, bf16[768]{0:T(1024)(128)(2,1)}, u32[]{:S(2)}) copy-start(bf16[768]{0:T(1024)(128)(2,1)} %get-tuple-element.55) | copy-start | bytes 4612
  392.8 36.0 %all-to-all-start.3 = ((bf16[8,128,640]{2,1,0:T(8,128)(2,1)}), bf16[8,128,640]{2,1,0:T(8,128)(2,1)S(1)}, u32[]{:S(2)}, u32[]{:S(2)}) async-start(bf16[8,128,640]{2,1,0:T(8,128)(2,1)} %bitcast.453), calls=%async_computation.3 | async-start | bytes 2621440 | tf_op jit(solution)/shard_map/all_to_all | solution.py:868
  396.6 148.0 %reduce-scatter.13.cloned.1.call-start = ((), (), s32[]{:S(2)}) async-start(), calls=%async_computation.19 | async-start | bytes 7618560 | tf_op jit(solution)/shard_map/reduce_scatter | solution.py:709
  442.7 190.7 %reduce-scatter.11.cloned.1.call-start = ((), (), s32[]{:S(2)}) async-start(), calls=%async_computation.18 | async-start | bytes 17694720 | tf_op jit(solution)/shard_map/reduce_scatter | solution.py:709
  455.1 36.0 %copy-start.28 = (bf16[768,1536]{1,0:T(8,128)(2,1)S(1)}, bf16[768,1536]{1,0:T(8,128)(2,1)}, u32[]{:S(2)}) copy-start(bf16[768,1536]{1,0:T(8,128)(2,1)} %all-gather.12.cloned.1.call-done.w_ref) | copy-start | bytes 7077892
  457.3 17.8 %collective-permute-start.10 = (bf16[96,3840]{1,0:T(8,128)(2,1)}, bf16[96,3840]{1,0:T(8,128)(2,1)}, u32[]{:S(2)}, u32[]{:S(2)}) collective-permute-start(bf16[96,3840]{1,0:T(8,128)(2,1)} %constant_dynamic-slice_fusion.8), channel_id=1, source_target_pairs={{0,4},{4,0},{8,12},{12,8},{16,20},{20,16},{24,28},{28,24},{1,5},{5... | collective-permute-start | bytes 2211848 | tf_op jit(solution)/shard_map/ppermute | solution.py:696
  478.3 9.3 %collective-permute-start.11 = (bf16[48,3840]{1,0:T(8,128)(2,1)}, bf16[48,3840]{1,0:T(8,128)(2,1)}, u32[]{:S(2)}, u32[]{:S(2)}) collective-permute-start(bf16[48,3840]{1,0:T(8,128)(2,1)} %constant_dynamic-slice_fusion.7), channel_id=1, source_target_pairs={{0,8},{4,12},{8,0},{12,4},{16,24},{20,28},{24,16},{28,20},{1,9},{5... | collective-permute-start | bytes 1105928 | tf_op jit(solution)/shard_map/ppermute | solution.py:696
  488.9 9.2 %collective-permute-start.12 = (bf16[24,3840]{1,0:T(8,128)(2,1)S(1)}, bf16[24,3840]{1,0:T(8,128)(2,1)S(1)}, u32[]{:S(2)}, u32[]{:S(2)}) collective-permute-start(bf16[24,3840]{1,0:T(8,128)(2,1)S(1)} %constant_dynamic-slice_fusion.6), channel_id=1, source_target_pairs={{0,16},{4,20},{8,24},{12,28},{16,0},{20,4},{24,8},{28,12},{1,17},{... | collective-permute-start | bytes 552968 | tf_op jit(solution)/shard_map/ppermute | solution.py:696
  498.2 10.0 %collective-permute-start.13 = (bf16[24,3840]{1,0:T(8,128)(2,1)S(1)}, bf16[24,3840]{1,0:T(8,128)(2,1)S(1)}, u32[]{:S(2)}, u32[]{:S(2)}) collective-permute-start(bf16[24,3840]{1,0:T(8,128)(2,1)S(1)} %get-tuple-element.72), channel_id=1, source_target_pairs={{0,16},{4,20},{8,24},{12,28},{16,0},{20,4},{24,8},{28,12},{1,17},{... | collective-permute-start | bytes 552968 | tf_op jit(solution)/shard_map/ppermute | solution.py:701
  508.1 10.4 %collective-permute-start.14 = (bf16[48,3840]{1,0:T(8,128)(2,1)S(1)}, bf16[48,3840]{1,0:T(8,128)(2,1)S(1)}, u32[]{:S(2)}, u32[]{:S(2)}) collective-permute-start(bf16[48,3840]{1,0:T(8,128)(2,1)S(1)} %constant_dynamic-update-slice_fusion.16), channel_id=1, source_target_pairs={{0,8},{4,12},{8,0},{12,4},{16,24},{20,28},{24,16},{28,20},{1,9},{5... | collective-permute-start | bytes 1105928 | tf_op jit(solution)/shard_map/ppermute | solution.py:701
  508.3 24.0 %copy-start.59 = (bf16[1152,768]{1,0:T(8,128)(2,1)S(1)}, bf16[1152,768]{1,0:T(8,128)(2,1)}, u32[]{:S(2)}) copy-start(bf16[1152,768]{1,0:T(8,128)(2,1)} %reduce-scatter.9.cloned.1.call-done) | copy-start | bytes 5308420
  509.6 22.6 %collective-permute-start.16 = (bf16[576,768]{1,0:T(8,128)(2,1)S(1)}, bf16[576,768]{1,0:T(8,128)(2,1)S(1)}, u32[]{:S(2)}, u32[]{:S(2)}) collective-permute-start(bf16[576,768]{1,0:T(8,128)(2,1)S(1)} %constant_dynamic-slice_fusion.5), channel_id=1, source_target_pairs={{0,4},{4,0},{8,12},{12,8},{16,20},{20,16},{24,28},{28,24},{1,5},{5... | collective-permute-start | bytes 2654216 | tf_op jit(solution)/shard_map/ppermute | solution.py:696
  518.6 34.4 %collective-permute-start.15 = (bf16[96,3840]{1,0:T(8,128)(2,1)S(1)}, bf16[96,3840]{1,0:T(8,128)(2,1)}, u32[]{:S(2)}, u32[]{:S(2)}) collective-permute-start(bf16[96,3840]{1,0:T(8,128)(2,1)S(1)} %constant_dynamic-update-slice_fusion.14), channel_id=1, source_target_pairs={{0,4},{4,0},{8,12},{12,8},{16,20},{20,16},{24,28},{28,24},{1,5},{5... | collective-permute-start | bytes 2211848 | tf_op jit(solution)/shard_map/ppermute | solution.py:701
  532.5 10.0 %collective-permute-start.17 = (bf16[288,768]{1,0:T(8,128)(2,1)S(1)}, bf16[288,768]{1,0:T(8,128)(2,1)S(1)}, u32[]{:S(2)}, u32[]{:S(2)}) collective-permute-start(bf16[288,768]{1,0:T(8,128)(2,1)S(1)} %constant_dynamic-slice_fusion.4), channel_id=1, source_target_pairs={{0,8},{4,12},{8,0},{12,4},{16,24},{20,28},{24,16},{28,20},{1,9},{5... | collective-permute-start | bytes 1327112 | tf_op jit(solution)/shard_map/ppermute | solution.py:696
  542.7 10.1 %collective-permute-start.18 = (bf16[144,768]{1,0:T(8,128)(2,1)S(1)}, bf16[144,768]{1,0:T(8,128)(2,1)S(1)}, u32[]{:S(2)}, u32[]{:S(2)}) collective-permute-start(bf16[144,768]{1,0:T(8,128)(2,1)S(1)} %constant_dynamic-slice_fusion.3), channel_id=1, source_target_pairs={{0,16},{4,20},{8,24},{12,28},{16,0},{20,4},{24,8},{28,12},{1,17},{... | collective-permute-start | bytes 663560 | tf_op jit(solution)/shard_map/ppermute | solution.py:696
  546.7 90.0 %collective-permute-start.4 = (bf16[96,3968]{1,0:T(8,128)(2,1)}, bf16[96,3968]{1,0:T(8,128)(2,1)}, u32[]{:S(2)}, u32[]{:S(2)}) collective-permute-start(bf16[96,3968]{1,0:T(8,128)(2,1)} %constant_dynamic-slice_fusion.11), channel_id=1, source_target_pairs={{0,4},{4,0},{8,12},{12,8},{16,20},{20,16},{24,28},{28,24},{1,5},{5... | collective-permute-start | bytes 2285576 | tf_op jit(solution)/shard_map/ppermute | solution.py:696
  552.9 11.4 %collective-permute-start.19 = (bf16[144,768]{1,0:T(8,128)(2,1)S(1)}, bf16[144,768]{1,0:T(8,128)(2,1)S(1)}, u32[]{:S(2)}, u32[]{:S(2)}) collective-permute-start(bf16[144,768]{1,0:T(8,128)(2,1)S(1)} %get-tuple-element.70), channel_id=1, source_target_pairs={{0,16},{4,20},{8,24},{12,28},{16,0},{20,4},{24,8},{28,12},{1,17},{... | collective-permute-start | bytes 663560 | tf_op jit(solution)/shard_map/ppermute | solution.py:701
  556.9 79.8 %copy-start.62 = (bf16[192,3968]{1,0:T(8,128)(2,1)S(1)}, bf16[192,3968]{1,0:T(8,128)(2,1)}, u32[]{:S(2)}) copy-start(bf16[192,3968]{1,0:T(8,128)(2,1)} %reduce-scatter.13.cloned.1.call-done) | copy-start | bytes 4571140
  564.3 75.3 %collective-permute-start.20 = (bf16[288,768]{1,0:T(8,128)(2,1)S(1)}, bf16[288,768]{1,0:T(8,128)(2,1)S(1)}, u32[]{:S(2)}, u32[]{:S(2)}) collective-permute-start(bf16[288,768]{1,0:T(8,128)(2,1)S(1)} %constant_dynamic-update-slice_fusion.10), channel_id=1, source_target_pairs={{0,8},{4,12},{8,0},{12,4},{16,24},{20,28},{24,16},{28,20},{1,9},{5... | collective-permute-start | bytes 1327112 | tf_op jit(solution)/shard_map/ppermute | solution.py:701
  635.0 41.6 %collective-permute-start.22 = (bf16[576,1536]{1,0:T(8,128)(2,1)S(1)}, bf16[576,1536]{1,0:T(8,128)(2,1)S(1)}, u32[]{:S(2)}, u32[]{:S(2)}) collective-permute-start(bf16[576,1536]{1,0:T(8,128)(2,1)S(1)} %constant_dynamic-slice_fusion.2), channel_id=1, source_target_pairs={{0,4},{4,0},{8,12},{12,8},{16,20},{20,16},{24,28},{28,24},{1,5},{5... | collective-permute-start | bytes 5308424 | tf_op jit(solution)/shard_map/ppermute | solution.py:696
  638.0 38.6 %copy-start.49 = (bf16[3,384,1536]{2,1,0:T(8,128)(2,1)S(1)}, bf16[3,384,1536]{2,1,0:T(8,128)(2,1)}, u32[]{:S(2)}) copy-start(bf16[3,384,1536]{2,1,0:T(8,128)(2,1)} %reduce-scatter.11.cloned.1.call-done) | copy-start | bytes 10616836
  638.1 40.6 %collective-permute-start.5 = (bf16[48,3968]{1,0:T(8,128)(2,1)S(1)}, bf16[48,3968]{1,0:T(8,128)(2,1)S(1)}, u32[]{:S(2)}, u32[]{:S(2)}) collective-permute-start(bf16[48,3968]{1,0:T(8,128)(2,1)S(1)} %constant_dynamic-slice_fusion.10), channel_id=1, source_target_pairs={{0,8},{4,12},{8,0},{12,4},{16,24},{20,28},{24,16},{28,20},{1,9},{5... | collective-permute-start | bytes 1142792 | tf_op jit(solution)/shard_map/ppermute | solution.py:696
  639.6 109.3 %collective-permute-start.21 = (bf16[576,768]{1,0:T(8,128)(2,1)S(1)}, bf16[576,768]{1,0:T(8,128)(2,1)S(1)}, u32[]{:S(2)}, u32[]{:S(2)}) collective-permute-start(bf16[576,768]{1,0:T(8,128)(2,1)S(1)} %constant_dynamic-update-slice_fusion.8), channel_id=1, source_target_pairs={{0,4},{4,0},{8,12},{12,8},{16,20},{20,16},{24,28},{28,24},{1,5},{5... | collective-permute-start | bytes 2654216 | tf_op jit(solution)/shard_map/ppermute | solution.py:701
  677.1 23.5 %collective-permute-start.23 = (bf16[288,1536]{1,0:T(8,128)(2,1)S(1)}, bf16[288,1536]{1,0:T(8,128)(2,1)S(1)}, u32[]{:S(2)}, u32[]{:S(2)}) collective-permute-start(bf16[288,1536]{1,0:T(8,128)(2,1)S(1)} %constant_dynamic-slice_fusion.1), channel_id=1, source_target_pairs={{0,8},{4,12},{8,0},{12,4},{16,24},{20,28},{24,16},{28,20},{1,9},{5... | collective-permute-start | bytes 2654216 | tf_op jit(solution)/shard_map/ppermute | solution.py:696
  678.8 23.6 %collective-permute-start.6 = (bf16[24,3968]{1,0:T(8,128)(2,1)S(1)}, bf16[24,3968]{1,0:T(8,128)(2,1)S(1)}, u32[]{:S(2)}, u32[]{:S(2)}) collective-permute-start(bf16[24,3968]{1,0:T(8,128)(2,1)S(1)} %constant_dynamic-slice_fusion.9), channel_id=1, source_target_pairs={{0,16},{4,20},{8,24},{12,28},{16,0},{20,4},{24,8},{28,12},{1,17},{... | collective-permute-start | bytes 571400 | tf_op jit(solution)/shard_map/ppermute | solution.py:696
  700.9 26.1 %collective-permute-start.24 = (bf16[144,1536]{1,0:T(8,128)(2,1)S(1)}, bf16[144,1536]{1,0:T(8,128)(2,1)S(1)}, u32[]{:S(2)}, u32[]{:S(2)}) collective-permute-start(bf16[144,1536]{1,0:T(8,128)(2,1)S(1)} %constant_dynamic-slice_fusion), channel_id=1, source_target_pairs={{0,16},{4,20},{8,24},{12,28},{16,0},{20,4},{24,8},{28,12},{1,17},{... | collective-permute-start | bytes 1327112 | tf_op jit(solution)/shard_map/ppermute | solution.py:696
  702.6 38.1 %collective-permute-start.7 = (bf16[24,3968]{1,0:T(8,128)(2,1)S(1)}, bf16[24,3968]{1,0:T(8,128)(2,1)S(1)}, u32[]{:S(2)}, u32[]{:S(2)}) collective-permute-start(bf16[24,3968]{1,0:T(8,128)(2,1)S(1)} %get-tuple-element.74), channel_id=1, source_target_pairs={{0,16},{4,20},{8,24},{12,28},{16,0},{20,4},{24,8},{28,12},{1,17},{... | collective-permute-start | bytes 571400 | tf_op jit(solution)/shard_map/ppermute | solution.py:701
  727.2 21.5 %collective-permute-start.25 = (bf16[144,1536]{1,0:T(8,128)(2,1)S(1)}, bf16[144,1536]{1,0:T(8,128)(2,1)S(1)}, u32[]{:S(2)}, u32[]{:S(2)}) collective-permute-start(bf16[144,1536]{1,0:T(8,128)(2,1)S(1)} %get-tuple-element.68), channel_id=1, source_target_pairs={{0,16},{4,20},{8,24},{12,28},{16,0},{20,4},{24,8},{28,12},{1,17},{... | collective-permute-start | bytes 1327112 | tf_op jit(solution)/shard_map/ppermute | solution.py:701
  740.7 16.2 %collective-permute-start.8 = (bf16[48,3968]{1,0:T(8,128)(2,1)S(1)}, bf16[48,3968]{1,0:T(8,128)(2,1)S(1)}, u32[]{:S(2)}, u32[]{:S(2)}) collective-permute-start(bf16[48,3968]{1,0:T(8,128)(2,1)S(1)} %constant_dynamic-update-slice_fusion.22), channel_id=1, source_target_pairs={{0,8},{4,12},{8,0},{12,4},{16,24},{20,28},{24,16},{28,20},{1,9},{5... | collective-permute-start | bytes 1142792 | tf_op jit(solution)/shard_map/ppermute | solution.py:701
  748.8 27.0 %collective-permute-start.26 = (bf16[288,1536]{1,0:T(8,128)(2,1)S(1)}, bf16[288,1536]{1,0:T(8,128)(2,1)S(1)}, u32[]{:S(2)}, u32[]{:S(2)}) collective-permute-start(bf16[288,1536]{1,0:T(8,128)(2,1)S(1)} %constant_dynamic-update-slice_fusion.4), channel_id=1, source_target_pairs={{0,8},{4,12},{8,0},{12,4},{16,24},{20,28},{24,16},{28,20},{1,9},{5... | collective-permute-start | bytes 2654216 | tf_op jit(solution)/shard_map/ppermute | solution.py:701
  756.9 21.7 %collective-permute-start.9 = (bf16[96,3968]{1,0:T(8,128)(2,1)S(1)}, bf16[96,3968]{1,0:T(8,128)(2,1)S(1)}, u32[]{:S(2)}, u32[]{:S(2)}) collective-permute-start(bf16[96,3968]{1,0:T(8,128)(2,1)S(1)} %constant_dynamic-update-slice_fusion.20), channel_id=1, source_target_pairs={{0,4},{4,0},{8,12},{12,8},{16,20},{20,16},{24,28},{28,24},{1,5},{5... | collective-permute-start | bytes 2285576 | tf_op jit(solution)/shard_map/ppermute | solution.py:701
  775.8 40.6 %collective-permute-start.27 = (bf16[576,1536]{1,0:T(8,128)(2,1)S(1)}, bf16[576,1536]{1,0:T(8,128)(2,1)S(1)}, u32[]{:S(2)}, u32[]{:S(2)}) collective-permute-start(bf16[576,1536]{1,0:T(8,128)(2,1)S(1)} %constant_dynamic-update-slice_fusion.2), channel_id=1, source_target_pairs={{0,4},{4,0},{8,12},{12,8},{16,20},{20,16},{24,28},{28,24},{1,5},{5... | collective-permute-start | bytes 5308424 | tf_op jit(solution)/shard_map/ppermute | solution.py:701
  (82 other events, 238.6 us)
Sparse Core Ops, SparseCore 0:
  9.6 33.4 all-gather.9
  44.6 24.5 all-gather.11
  70.8 17.4 all-gather.13
  89.8 37.4 all-gather.15
  128.6 37.4 all-gather.17
  167.5 17.4 all-gather.21
  186.6 17.4 all-gather.19
  205.6 91.0 all-gather.23
  338.3 56.6 reduce-scatter.6
  398.1 63.6 reduce-scatter.8
  464.3 57.0 reduce-scatter.12
  524.0 109.3 reduce-scatter.10
